TPU v7x, 256 devices: a whole 4x4x8 slice. The times are simulated.
256 devices in a mesh: shell: 128 (over x, y, z), radial: 2 (over core).
Axes of the slice: x: 4, y: 4, z: 8, core: 2. Of those that a mesh axis runs over, the one named last changes fastest.
Arguments:
- state: float32 [8, 32, 1024, 128], P(None, 'radial', 'shell')
- footpoints: int32 [32, 1024, 128], P('radial', 'shell'), may hold values from 0 to 32767, as said below
- conductance: float32 [4, 128, 256], P(None, 'shell', 'radial'), may hold values from 0.1 to 0.45
- inverse_blocks: float32 [128, 2, 128, 128], P('shell', 'radial')
Outputs:
- state_next: float32 [8, 32, 1024, 128], P(None, 'radial', 'shell')
- potential: float32 [128, 256], P('shell', 'radial')
- footpoint_potential: float32 [32, 1024, 128], P('radial', 'shell')
Inputs may be any that keep to these rules, and one draw needn't show every extreme that they name: `footpoints`: A cell whose longitude index lon lies in shell block s = lon // 8 maps to a node whose column (node % 256) lies in s * 2 to (s + 1) * 2 - 1.
All inputs are finite; a program needn't handle non-finite values.
Results may differ from a plain program's by a relative error of at most 0.0003.
Values sent between devices are 32-bit elements; how exact they have to be, the bound alone decides.
A program may use at most 64 MiB of HBM per device.

v0:
```python
import jax
import jax.numpy as jnp
from jax import lax
from jax.sharding import PartitionSpec as P

NLAT_I = 128
NLON_I = 256
ITERS_I = 4


GAMMA = 5.0 / 3.0
TIME_STEP = 0.02
CELL_AREA = 0.125


def padded_2(block, sides, width, periodic):
    for axis, dim in sides:
        count = lax.axis_size(axis)
        forward = [(i, i + 1) for i in range(count - 1)]
        if periodic:
            forward.append((count - 1, 0))
        backward = [(target, source) for source, target in forward]
        low = lax.ppermute(
            lax.slice_in_dim(block, block.shape[dim] - width, None, axis=dim), axis, forward
        )
        high = lax.ppermute(lax.slice_in_dim(block, 0, width, axis=dim), axis, backward)
        block = jnp.concatenate([low, block, high], axis=dim)
    return block


def minmod(first_jump, second_jump):
    return (
        0.5
        * (jnp.sign(first_jump) + jnp.sign(second_jump))
        * jnp.minimum(jnp.abs(first_jump), jnp.abs(second_jump))
    )


def physical_flux(conserved, direction):
    density = conserved[0]
    velocity = conserved[1:4] / density
    magnetic = conserved[4:7]
    energy = conserved[7]
    field_sq = jnp.sum(magnetic * magnetic, axis=0)
    kinetic = jnp.sum(velocity * velocity, axis=0)
    pressure = (GAMMA - 1.0) * (energy - 0.5 * density * kinetic - 0.5 * field_sq)
    total_pressure = pressure + 0.5 * field_sq
    normal_speed = velocity[direction]
    normal_field = magnetic[direction]
    selector = (jnp.arange(3) == direction).astype(jnp.float32).reshape((3,) + (1,) * density.ndim)
    momentum_flux = (
        density * velocity * normal_speed - magnetic * normal_field + total_pressure * selector
    )
    induction = normal_speed * magnetic - normal_field * velocity
    alignment = jnp.sum(velocity * magnetic, axis=0)
    energy_flux = (energy + total_pressure) * normal_speed - normal_field * alignment
    fluxes = jnp.concatenate(
        [(density * normal_speed)[None], momentum_flux, induction, energy_flux[None]], axis=0
    )
    signal = jnp.abs(normal_speed) + jnp.sqrt((GAMMA * jnp.abs(pressure) + field_sq) / density)
    return (fluxes, signal)


def face_divergence(padded, direction):
    dimension = direction + 1
    cell_count = padded.shape[dimension] - 4

    def window_slice(array, first_index, length):
        return lax.slice_in_dim(array, first_index, first_index + length, axis=dimension)

    jumps = window_slice(padded, 1, cell_count + 3) - window_slice(padded, 0, cell_count + 3)
    slopes = minmod(window_slice(jumps, 1, cell_count + 2), window_slice(jumps, 0, cell_count + 2))
    left_state = window_slice(padded, 1, cell_count + 1) + 0.5 * window_slice(
        slopes, 0, cell_count + 1
    )
    right_state = window_slice(padded, 2, cell_count + 1) - 0.5 * window_slice(
        slopes, 1, cell_count + 1
    )
    left_flux, left_signal = physical_flux(left_state, direction)
    right_flux, right_signal = physical_flux(right_state, direction)
    signal_max = jnp.maximum(left_signal, right_signal)
    face_flux = 0.5 * (left_flux + right_flux) - 0.5 * signal_max * (right_state - left_state)
    return window_slice(face_flux, 1, cell_count) - window_slice(face_flux, 0, cell_count)


def tendency(padded):
    total_div = face_divergence(padded[:, :, 2:-2, 2:-2], 0)
    total_div = total_div + face_divergence(padded[:, 2:-2, :, 2:-2], 1)
    total_div = total_div + face_divergence(padded[:, 2:-2, 2:-2, :], 2)
    return -total_div


def shifted(values, direction, offset):
    for dimension in range(3):
        first_index = offset if dimension == direction else 2
        length = values.shape[dimension] - 4
        values = lax.slice_in_dim(values, first_index, first_index + length, axis=dimension)
    return values


def field_current(padded):
    magnetic = padded[4:7]

    def derivative(component, direction):
        return 0.5 * (
            shifted(magnetic[component], direction, 3) - shifted(magnetic[component], direction, 1)
        )

    curl_first = derivative(2, 1) - derivative(1, 2)
    curl_second = derivative(0, 2) - derivative(2, 0)
    curl_third = derivative(1, 0) - derivative(0, 1)
    centre = [shifted(magnetic[component], 0, 2) for component in range(3)]
    field_sq = centre[0] * centre[0] + centre[1] * centre[1] + centre[2] * centre[2]
    aligned = curl_first * centre[0] + curl_second * centre[1] + curl_third * centre[2]
    return CELL_AREA * aligned / jnp.sqrt(1.0 + field_sq)


def pad_latitude(field):
    return jnp.pad(field, ((0, 0), (0, 0), (0, 0), (2, 2)), mode="edge")


def fill_radial(field, margin):
    position = lax.axis_index("radial")
    last_index = lax.axis_size("radial") - 1
    extent = field.shape[1]
    layer_index = lax.broadcasted_iota(jnp.int32, (1, extent, 1, 1), 1)
    lower_edge = lax.slice_in_dim(field, margin, margin + 1, axis=1)
    upper_edge = lax.slice_in_dim(field, extent - margin - 1, extent - margin, axis=1)
    field = jnp.where((layer_index < margin) & (position == 0), lower_edge, field)
    return jnp.where((layer_index >= extent - margin) & (position == last_index), upper_edge, field)


def extended_cells(field):
    grown = padded_2(field, (("shell", 2), ("radial", 1)), 2, True)
    return pad_latitude(fill_radial(grown, 2))


def body(state, footpoints, conductance, inverse_blocks):
    first_padded = extended_cells(state)
    section_one = state + TIME_STEP * tendency(first_padded)
    second_padded = extended_cells(section_one)
    state_next = 0.5 * state + 0.5 * (section_one + TIME_STEP * tendency(second_padded))
    cell_current = field_current(first_padded).reshape(-1)
    rows_owned = inverse_blocks.shape[0]
    half_width = inverse_blocks.shape[2]
    halves_count = lax.axis_size("radial")
    latitude_node = footpoints // NLON_I
    column_node = footpoints % NLON_I
    owner_index = latitude_node // rows_owned * halves_count + column_node // half_width
    node_slot = (
        owner_index * (rows_owned * half_width)
        + latitude_node % rows_owned * half_width
        + column_node % half_width
    )
    partial_sums = jax.ops.segment_sum(
        cell_current, node_slot.reshape(-1), num_segments=NLAT_I * NLON_I
    )
    currents = lax.psum_scatter(
        partial_sums, ("shell", "radial"), scatter_dimension=0, tiled=True
    ).reshape(rows_owned, half_width)
    block_matrices = inverse_blocks[:, 0]

    def apply_blocks(vector):
        return jnp.einsum("rij,rj->ri", block_matrices, vector, precision=lax.Precision.HIGHEST)

    potential = apply_blocks(currents)
    for sweep_index in range(ITERS_I - 1):
        padded_panel = padded_2(potential, (("shell", 0), ("radial", 1)), 1, False)
        coupled = currents + conductance[0] * padded_panel[:-2, 1:-1]
        coupled = coupled + conductance[1] * padded_panel[2:, 1:-1]
        coupled = coupled + conductance[2] * padded_panel[1:-1, :-2]
        coupled = coupled + conductance[3] * padded_panel[1:-1, 2:]
        potential = apply_blocks(coupled)
    whole_table = lax.all_gather(potential.reshape(-1), ("shell", "radial"), axis=0, tiled=True)
    footpoint_potential = whole_table[node_slot]
    return (state_next, potential, footpoint_potential)


def solution(mesh):
    return jax.shard_map(
        body,
        mesh=mesh,
        in_specs=(
            P(None, "radial", "shell", None),
            P("radial", "shell", None),
            P(None, "shell", "radial"),
            P("shell", "radial", None, None),
        ),
        out_specs=(
            P(None, "radial", "shell", None),
            P("shell", "radial"),
            P("radial", "shell", None),
        ),
        check_vma=False,
    )
```

profile of v0, /device:TPU:1, one launch (start us, length us, event | category | flops | bytes accessed | tf_op | source)
XLA Modules:
  0.0 684.4 jit_solution(17312191880690666836)
XLA Ops:
  7.2 1.4 fusion.271
  8.6 2.5 collective-permute-start
  11.1 8.7 %collective-permute-start.1 = (f32[8,16,2,128]{3,2,1,0:T(2,128)S(1)}, f32[8,16,2,128]{3,2,1,0:T(2,128)S(1)}, u32[]{:S(2)}, u32[]{:S(2)}) collective-permute-start(f32[8,16,2,128]{3,2,1,0:T(2,128)S(1)} %get-tuple-element.179), channel_id=1, source_target_pairs={{2,0},{4,2},{6,4},{8,6},{10,8},{12,10},{14,12},{16,14},{18,16},{20... | collective-permute-start | bytes 393224 | tf_op jit(solution)/shard_map/ppermute | solution.py:26
  20.9 1.6 fusion.158
  28.9 1.6 fusion.269
  30.5 2.5 copy.843
  36.1 2.6 pad_maximum_fusion
  39.9 1.5 multiply_reduce_fusion.31
  42.6 1.8 multiply_reduce_fusion.22
  45.0 1.6 multiply_reduce_fusion.19
  49.1 86.8 %scatter_custom_fusion = f32[32768]{0:T(1024)} fusion(s32[16384]{0:T(1024)} %bitcast.618, f32[16384]{0:T(1024)} %bitcast.619, f32[]{:T(128)} %constant.97.clone.1), kind=kCustom, calls=%fused_computation.431 | custom fusion | flops 16384 | bytes 131584 | tf_op jit(solution)/shard_map/scatter-add | solution.py:155
  136.0 2.6 slice_subtract_fusion.1
  149.9 228.3 %all-reduce.3.cloned.1.call-done = f32[32768]{0:T(1024)} async-done(((f32[32768]{0:T(1024)}), f32[32768]{0:T(1024)}) %all-reduce.3.cloned.1.call-update) | async-done | bytes 131088
  380.5 4.4 collective-permute-start.8
  384.9 1.4 fusion.24
  387.7 4.2 collective-permute-start.11
  392.9 1.5 collective-permute-start.13
  394.4 4.3 collective-permute-start.12
  400.8 3.1 collective-permute-start.15
  406.3 4.5 collective-permute-start.16
  410.9 1.8 collective-permute-start.4
  412.7 5.2 collective-permute-start.5
  419.2 3.1 collective-permute-start.19
  423.4 61.8 %all-gather = f32[256,1,128]{2,1,0:T(1,128)S(1)} all-gather(f32[1,1,128]{2,1,0:T(1,128)S(1)} %bitcast.621), channel_id=1, replica_groups=mesh['shell'=128,'radial'=2] {'shell','radial'}, dimensions={0}, use_global_device_ids=true | all-gather | bytes 131584 | tf_op jit(solution)/shard_map/all_gather | solution.py:174
  485.1 160.6 %gather_fusion = f32[16384]{0:T(1024)} fusion(f32[32768]{0:T(1024)S(1)} %bitcast.598, s32[16384]{0:T(1024)S(1)} %copy-done.67), kind=kCustom, calls=%fused_computation | custom fusion | bytes 196608 | tf_op jit(solution)/shard_map/gather | solution.py:175
  648.2 1.9 fusion.268
  650.5 1.4 multiply_reduce_fusion.28
  652.0 1.4 multiply_reduce_fusion.25
  654.6 1.8 multiply_reduce_fusion.10
  657.0 1.6 multiply_reduce_fusion.7
  659.3 3.2 copy.860
  662.5 3.2 copy.861
  (292 shorter events, 55.3 us)
Async XLA Ops:
  7.2 371.8 %copy-start = (f32[1,1,128,128]{3,2,1,0:T(8,128)S(1)}, f32[1,1,128,128]{3,2,1,0:T(8,128)}, u32[]{:S(2)}) copy-start(f32[1,1,128,128]{3,2,1,0:T(8,128)} %param.7) | copy-start | bytes 196612
  7.2 18.3 %copy-start.4 = (f32[8,16,8,128]{3,2,1,0:T(8,128)S(1)}, f32[8,16,8,128]{3,2,1,0:T(8,128)}, u32[]{:S(2)}) copy-start(f32[8,16,8,128]{3,2,1,0:T(8,128)} %param.4) | copy-start | bytes 1572868
  7.2 371.0 %all-reduce.3.cloned.1.call-start = ((), (), s32[]{:S(2)}) async-start(), calls=%async_computation | async-start | bytes 262144
  8.6 14.5 %collective-permute-start = (f32[8,16,2,128]{3,2,1,0:T(2,128)S(1)}, f32[8,16,2,128]{3,2,1,0:T(2,128)S(1)}, u32[]{:S(2)}, u32[]{:S(2)}) collective-permute-start(f32[8,16,2,128]{3,2,1,0:T(2,128)S(1)} %get-tuple-element.178), channel_id=1, source_target_pairs={{0,2},{2,4},{4,6},{6,8},{8,10},{10,12},{12,14},{14,16},{16,18},{18... | collective-permute-start | bytes 393224 | tf_op jit(solution)/shard_map/ppermute | solution.py:23
  11.1 12.0 %collective-permute-start.1 = (f32[8,16,2,128]{3,2,1,0:T(2,128)S(1)}, f32[8,16,2,128]{3,2,1,0:T(2,128)S(1)}, u32[]{:S(2)}, u32[]{:S(2)}) collective-permute-start(f32[8,16,2,128]{3,2,1,0:T(2,128)S(1)} %get-tuple-element.179), channel_id=1, source_target_pairs={{2,0},{4,2},{6,4},{8,6},{10,8},{12,10},{14,12},{16,14},{18,16},{20... | collective-permute-start | bytes 393224 | tf_op jit(solution)/shard_map/ppermute | solution.py:26
  24.1 2.1 collective-permute-start.2
  25.2 1.3 collective-permute-start.3
  42.5 4.1 copy-start.9
  42.5 4.1 copy-start.11
  148.9 235.9 %copy-start.58 = (f32[17,8,128]{2,1,0:T(8,128)S(1)}, f32[17,8,128]{2,1,0:T(8,128)}, u32[]{:S(2)}) copy-start(f32[17,8,128]{2,1,0:T(8,128)} %get-tuple-element.83) | copy-start | bytes 208900
  379.1 7.2 %collective-permute-start.9 = (f32[1,128]{1,0:T(1,128)S(1)}, f32[1,128]{1,0:T(1,128)S(1)}, u32[]{:S(2)}, u32[]{:S(2)}) collective-permute-start(f32[1,128]{1,0:T(1,128)S(1)} %fusion.181), channel_id=1, source_target_pairs={{2,0},{4,2},{6,4},{8,6},{10,8},{12,10},{14,12},{16,14},{18,16},{20... | collective-permute-start | bytes 1544 | tf_op jit(solution)/shard_map/ppermute | solution.py:26
  380.5 5.9 collective-permute-start.8
  384.9 7.8 %copy-start.76 = (f32[4,1,128]{2,1,0:T(1,128)S(1)}, f32[4,1,128]{2,1,0:T(1,128)}, u32[]{:S(2)}) copy-start(f32[4,1,128]{2,1,0:T(1,128)} %param.6) | copy-start | bytes 6148
  384.9 13.8 %copy-start.19 = (f32[8,16,8,129]{3,2,1,0:T(8,128)S(1)}, f32[8,16,8,129]{3,2,1,0:T(8,128)}, u32[]{:S(2)}) copy-start(f32[8,16,8,129]{3,2,1,0:T(8,128)} %fusion.14) | copy-start | bytes 1585156
  386.4 5.5 collective-permute-start.10
  387.7 5.0 collective-permute-start.11
  392.9 92.2 %copy-start.67 = (s32[16384]{0:T(1024)S(1)}, s32[16384]{0:T(1024)}, u32[]{:S(2)}) copy-start(s32[16384]{0:T(1024)} %get-tuple-element.66) | copy-start | bytes 196612
  392.9 6.1 collective-permute-start.13
  394.4 5.1 collective-permute-start.12
  399.5 4.4 collective-permute-start.14
  400.8 3.9 collective-permute-start.15
  404.9 12.9 %collective-permute-start.17 = (f32[1,128]{1,0:T(1,128)S(1)}, f32[1,128]{1,0:T(1,128)S(1)}, u32[]{:S(2)}, u32[]{:S(2)}) collective-permute-start(f32[1,128]{1,0:T(1,128)S(1)} %fusion.177), channel_id=1, source_target_pairs={{2,0},{4,2},{6,4},{8,6},{10,8},{12,10},{14,12},{16,14},{18,16},{20... | collective-permute-start | bytes 1544 | tf_op jit(solution)/shard_map/ppermute | solution.py:26
  406.3 11.6 %collective-permute-start.16 = (f32[1,128]{1,0:T(1,128)S(1)}, f32[1,128]{1,0:T(1,128)S(1)}, u32[]{:S(2)}, u32[]{:S(2)}) collective-permute-start(f32[1,128]{1,0:T(1,128)S(1)} %fusion.177), channel_id=1, source_target_pairs={{0,2},{2,4},{4,6},{6,8},{8,10},{10,12},{12,14},{14,16},{16,18},{18... | collective-permute-start | bytes 1544 | tf_op jit(solution)/shard_map/ppermute | solution.py:23
  410.9 234.8 %collective-permute-start.4 = (f32[8,16,2,128]{3,2,1,0:T(2,128)S(1)}, f32[8,16,2,128]{3,2,1,0:T(2,128)S(1)}, u32[]{:S(2)}, u32[]{:S(2)}) collective-permute-start(f32[8,16,2,128]{3,2,1,0:T(2,128)S(1)} %get-tuple-element.176), channel_id=1, source_target_pairs={{0,2},{2,4},{4,6},{6,8},{8,10},{10,12},{12,14},{14,16},{16,18},{18... | collective-permute-start | bytes 393224 | tf_op jit(solution)/shard_map/ppermute | solution.py:23
  412.7 233.0 %collective-permute-start.5 = (f32[8,16,2,128]{3,2,1,0:T(2,128)S(1)}, f32[8,16,2,128]{3,2,1,0:T(2,128)S(1)}, u32[]{:S(2)}, u32[]{:S(2)}) collective-permute-start(f32[8,16,2,128]{3,2,1,0:T(2,128)S(1)} %get-tuple-element.177), channel_id=1, source_target_pairs={{2,0},{4,2},{6,4},{8,6},{10,8},{12,10},{14,12},{16,14},{18,16},{20... | collective-permute-start | bytes 393224 | tf_op jit(solution)/shard_map/ppermute | solution.py:26
  418.0 4.4 collective-permute-start.18
  419.2 3.9 collective-permute-start.19
  423.4 222.4 %copy-start.75 = (f32[1,128]{1,0:T(1,128)}, f32[1,128]{1,0:T(1,128)S(1)}, u32[]{:S(2)}) copy-start(f32[1,128]{1,0:T(1,128)S(1)} %fusion.175) | copy-start | bytes 1540
  645.8 1.4 collective-permute-start.6
  646.1 1.5 collective-permute-start.7
  654.6 4.1 copy-start.5
  654.6 4.1 copy-start.7
  (66 other events, 114.2 us)
Sparse Core Ops, SparseCore 0:
  136.1 242.0 all-reduce.2
where the time goes:
time: 685 us; the launch traced here: 684 us
  waiting for transfers between devices  233 us (34%)
  local copies, waits for them, and re-layouts  191 us (28%)
  other arithmetic  131 us (19%)
  blocking collectives  61.8 us (9%)
  starting transfers between devices  51.8 us (8%)
  between operations  15.3 us (2%)
    unnamed x2, waiting for transfers between devices  228 us
    gather x1, local copies, waits for them, and re-layouts, body(): footpoint_potential = whole_table[node_slot]  161 us
    scatter-add x1, other arithmetic, body(): jax.ops.segment_sum(cell_current, node_slot.reshape(-1), num_segments=NLA...  86.8 us
    all_gather x1, blocking collectives, body(): lax.all_gather(potential.reshape(-1), ('shell', 'radial'), axis=0, tiled=...  61.8 us
    ppermute x10, starting transfers between devices, padded_2(): lax.ppermute(lax.slice_in_dim(block, 0, width, axis=dim), axis, backward)  28.9 us
    ppermute x10, starting transfers between devices, padded_2(): lax.ppermute(lax.slice_in_dim(block, block.shape[dim] - width, None, axis...  22.8 us
  transfers between devices with their start and end apart: 21, of which 9 were waited for; matrix products, arithmetic and copies ran while one was open for 26% of the time, Pallas kernels for 0%

commit v1 on v0

v1 whole, which is shorter than its diff:
```python
import jax
import jax.numpy as jnp
from jax import lax
from jax.experimental import pallas as pl
from jax.experimental.pallas import tpu as pltpu
from jax.sharding import PartitionSpec as P

F32 = jnp.float32
BF16 = jnp.bfloat16
GAMMA = 5.0 / 3.0
TIME_STEP = 0.02
CELL_AREA = 0.125
SWEEPS = 4

NZ = 8
NXY = 16
R = 16
LON = 8
LAT = 128
FAR_FIRST_Z = (4, 3, 5, 2, 6, 1, 7)
FAR_FIRST_XY = (10, 6, 14, 2, 9, 11, 5, 7, 13, 15, 1, 3, 8, 4, 12)

NT = (((1,), (1,)), ((), ()))
MESH = pl.DeviceIdType.MESH


def minmod(a, b):
    return jnp.maximum(jnp.minimum(a, jnp.maximum(b, 0.0)), jnp.minimum(b, 0.0))


def flux(u, d):
    density, energy = u[0], u[7]
    inv = 1.0 / density
    vel = [u[1] * inv, u[2] * inv, u[3] * inv]
    mag = u[4:7]
    field_sq = mag[0] * mag[0] + mag[1] * mag[1] + mag[2] * mag[2]
    kinetic = vel[0] * vel[0] + vel[1] * vel[1] + vel[2] * vel[2]
    half_sq = 0.5 * field_sq
    pressure = (GAMMA - 1.0) * (energy - 0.5 * density * kinetic - half_sq)
    total = pressure + half_sq
    vn, bn = vel[d], mag[d]
    align = vel[0] * mag[0] + vel[1] * mag[1] + vel[2] * mag[2]
    out = [u[1 + d]]
    for k in range(3):
        m = u[1 + k] * vn - mag[k] * bn
        out.append(m + total if k == d else m)
    for k in range(3):
        out.append(None if k == d else vn * mag[k] - bn * vel[k])
    out.append((energy + total) * vn - bn * align)
    signal = jnp.abs(vn) + jnp.sqrt((GAMMA * jnp.abs(pressure) + field_sq) * inv)
    return out, signal


def face(left, right, d):
    fl, sl = flux(left, d)
    fr, sr = flux(right, d)
    top = jnp.maximum(sl, sr)
    out = []
    for k in range(8):
        jump = top * (right[k] - left[k])
        out.append(-jump if fl[k] is None else (fl[k] + fr[k]) - jump)
    return out


def split2(x):
    hi = x.astype(BF16)
    lo = (x - hi.astype(F32)).astype(BF16)
    return hi, lo


def nt(a, b):
    return lax.dot_general(a, b, NT, preferred_element_type=F32)


def lat_pass(src, base, acc):
    lane = lax.broadcasted_iota(jnp.int32, (2, LON, LAT), 2)
    last, first = lane == LAT - 1, lane == 0

    def step(i, carry):
        l = i * 2
        left, right = [], []
        for v in range(8):
            u = src[v, pl.ds(base + l, 2)]
            d = jnp.where(last, 0.0, pltpu.roll(u, LAT - 1, 2) - u)
            h = 0.5 * minmod(d, pltpu.roll(d, 1, 2))
            left.append(u + h)
            r = u - h
            right.append(jnp.where(last, r, pltpu.roll(r, LAT - 1, 2)))
        fl, sl = flux(left, 2)
        fr, sr = flux(right, 2)
        top = jnp.maximum(sl, sr)
        for v in range(8):
            jump = top * (right[v] - left[v])
            if fl[v] is None:
                f = -jump
                acc[v, pl.ds(l, 2)] = f - jnp.where(first, 0.0, pltpu.roll(f, 1, 2))
            else:
                f = (fl[v] + fr[v]) - jump
                acc[v, pl.ds(l, 2)] = f - jnp.where(first, 2.0 * fl[v], pltpu.roll(f, 1, 2))
        return carry

    lax.fori_loop(0, R // 2, step, 0)


def radial_pass(ext, acc):
    half = R // 2

    def cells(i):
        return [jnp.stack([ext[v, i], ext[v, i + half]]) for v in range(8)]

    def advance(f, prev, here):
        nxt = cells(f + 2)
        left, right, jumps = [], [], []
        for v in range(8):
            d = nxt[v] - here[v]
            h = 0.5 * minmod(d, prev[v])
            jumps.append(d)
            left.append(here[v] + h)
            right.append(here[v] - h)
        return nxt, jumps, left, right

    c0, c1 = cells(0), cells(1)
    prev = [c1[v] - c0[v] for v in range(8)]
    here, prev, left, _ = advance(0, prev, c1)
    here, prev, left2, right = advance(1, prev, here)
    f0 = face(left, right, 0)

    def step(i, carry):
        here, prev, left, f0 = carry
        here, prev, left2, right = advance(i + 2, prev, here)
        f1 = face(left, right, 0)
        for v in range(8):
            df = f1[v] - f0[v]
            acc[v, i] += df[0]
            acc[v, i + half] += df[1]
        return here, prev, left2, f1

    lax.fori_loop(0, half, step, (here, prev, left2, f0))


def lon_pass(ext, acc):
    def advance(i, prev, here):
        left, right, jumps, nxt = [], [], [], []
        for v in range(8):
            n = ext[v, i]
            d = n - here[v]
            h = 0.5 * minmod(d, prev[v])
            nxt.append(n)
            jumps.append(d)
            left.append(here[v] + h)
            right.append(here[v] - h)
        return nxt, jumps, left, right

    c0 = [ext[v, 0] for v in range(8)]
    c1 = [ext[v, 1] for v in range(8)]
    prev = [c1[v] - c0[v] for v in range(8)]
    here, prev, left, _ = advance(2, prev, c1)
    here, prev, left2, right = advance(3, prev, here)
    f0 = face(left, right, 1)

    def step(i, carry):
        here, prev, left, f0 = carry
        here, prev, left2, right = advance(i + 4, prev, here)
        f1 = face(left, right, 1)
        for v in range(8):
            acc[v, i] = f1[v] - f0[v]
        return here, prev, left2, f1

    lax.fori_loop(0, LON, step, (here, prev, left2, f0))


def kernel(
    state, foot, cond, inv,
    out_state, out_pot, out_foot,
    xr, xt, yr, yt, acc, acct, dt1,
    part, zb, zs, ab, prow, sweep, zp, ps, ap,
    send_sem, recv_sem,
):
    s = lax.axis_index("shell")
    h = lax.axis_index("radial")
    z, xy = s % NZ, s // NZ
    base = s - z
    right = ((s + 1) % (NZ * NXY), h)
    left = ((s + NZ * NXY - 1) % (NZ * NXY), h)
    mate = (s, 1 - h)
    line = [(base + (z + k) % NZ, c) for k in FAR_FIRST_Z for c in (0, 1)] + [mate]
    plane = [((xy + k) % NXY * NZ + z, h) for k in FAR_FIRST_XY]
    slot = z * 2 + h

    def remote(src, dst, n, device):
        copy = pltpu.make_async_remote_copy(
            src_ref=src, dst_ref=dst, send_sem=send_sem.at[n], recv_sem=recv_sem.at[n],
            device_id=device, device_id_type=MESH,
        )
        copy.start()
        return copy

    def landed(ref, n):
        pltpu.make_async_copy(ref, ref, recv_sem.at[n]).wait()

    def sent(ref, n):
        pltpu.make_async_copy(ref, ref, send_sem.at[n]).wait()

    barrier = pltpu.get_barrier_semaphore()
    partners = line + plane + [right, left]
    for device in partners:
        pl.semaphore_signal(barrier, inc=1, device_id=device, device_id_type=MESH)

    for v in (4, 5, 6, 0, 1, 2, 3, 7):
        for j in range(LON):
            xt[v, j + 2] = state[v, :, j, :]
    edge, low = 18 * h, 14 * (1 - h)
    for v in range(8):
        xr[v, pl.ds(2, R)] = state[v]
        e = state[v, 15 * h]
        xr[v, edge] = e
        xr[v, edge + 1] = e
    inv_hi, inv_lo = split2(inv[0, 0])
    pl.semaphore_wait(barrier, len(partners))

    copies = []
    for n, lo, cnt in ((0, 4, 3), (3, 0, 4), (6, 7, 1)):
        vs = pl.ds(lo, cnt)
        copies.append(remote(state.at[vs, pl.ds(low, 2)], xr.at[vs, pl.ds(edge, 2)], n, mate))
        copies.append(remote(xt.at[vs, pl.ds(8, 2)], xt.at[vs, pl.ds(0, 2)], n + 1, right))
        copies.append(remote(xt.at[vs, pl.ds(2, 2)], xt.at[vs, pl.ds(10, 2)], n + 2, left))

    lat_pass(state, 0, acc)

    for c in copies[:3]:
        c.wait_recv()
    for k, v in enumerate((6, 4)):
        for j in range(LON):
            dt1[k, j] = xt[v, j + 3] - xt[v, j + 1]
    lane3 = lax.broadcasted_iota(jnp.int32, (LON, LAT), 1)
    first, last = lane3 == 0, lane3 == LAT - 1
    row16 = lax.broadcasted_iota(jnp.int32, (16, LAT), 0)

    def along_lat(b):
        up = jnp.where(last, b, pltpu.roll(b, LAT - 1, 1))
        down = jnp.where(first, b, pltpu.roll(b, 1, 1))
        return up - down

    def current_step(l, total):
        b = [xr[v, l + 2] for v in (4, 5, 6)]
        up = [xr[v, l + 3] for v in (5, 6)]
        dn = [xr[v, l + 1] for v in (5, 6)]
        c0 = dt1[0, :, l, :] - along_lat(b[1])
        c1 = along_lat(b[0]) - (up[1] - dn[1])
        c2 = (up[0] - dn[0]) - dt1[1, :, l, :]
        sq = b[0] * b[0] + b[1] * b[1] + b[2] * b[2]
        val = (0.5 * CELL_AREA) * (c0 * b[0] + c1 * b[1] + c2 * b[2]) / jnp.sqrt(1.0 + sq)
        hi = val.astype(BF16).astype(F32)
        lo = (val - hi).astype(BF16).astype(F32)
        node = foot[l]
        row = jnp.right_shift(node, 8)
        group = jnp.bitwise_and(node, 1) * 8 + jnp.right_shift(row, 4)
        inner = jnp.bitwise_and(row, 15)
        a, bmat = [], []
        for j in range(LON):
            hit = jnp.broadcast_to(group[j : j + 1], (16, LAT)) == row16
            a.append(
                jnp.concatenate(
                    [
                        jnp.where(hit, jnp.broadcast_to(hi[j : j + 1], (16, LAT)), 0.0).astype(BF16),
                        jnp.where(hit, jnp.broadcast_to(lo[j : j + 1], (16, LAT)), 0.0).astype(BF16),
                    ],
                    axis=0,
                )
            )
            one = jnp.where(jnp.broadcast_to(inner[j : j + 1], (16, LAT)) == row16, 1.0, 0.0)
            bmat.append(jnp.concatenate([one.astype(BF16)] * 8, axis=0))
        return total + nt(jnp.concatenate(a, axis=1), jnp.concatenate(bmat, axis=1))

    total = lax.fori_loop(0, R, current_step, jnp.zeros((32, LAT), F32))
    total = total[:16] + total[16:]
    lane16 = lax.broadcasted_iota(jnp.int32, (16, LAT), 1)
    total = jnp.where(jnp.right_shift(lane16, 4) == jnp.bitwise_and(row16, 7), total, 0.0)
    mine = jnp.concatenate(
        [jnp.sum(total[:8], axis=0, keepdims=True), jnp.sum(total[8:], axis=0, keepdims=True)], axis=0
    )
    part[...] = mine
    zb[slot] = mine
    for device in line:
        remote(part, zb.at[slot], 9, device)

    for c in copies[3:]:
        c.wait_recv()
    radial_pass(xr, acc)

    landed(zb.at[pl.ds(0, 15)], 9)
    for k in range(NZ):
        zs[2 * k : 2 * k + 2, :] = zb[2 * k] + zb[2 * k + 1]
    ab[xy] = zs[...]
    for device in plane:
        remote(zs, ab.at[xy], 10, device)

    lon_pass(xt, acct)

    def section_one(l, carry):
        for v in range(8):
            yr[v, l + 2] = state[v, l] - (0.5 * TIME_STEP) * (acc[v, l] + acct[v, :, l, :])
        return carry

    lax.fori_loop(0, R, section_one, 0)
    for v in range(8):
        for j in range(LON):
            yt[v, j + 2] = yr[v, 2 : R + 2, j, :]
        e = yr[v, 2 + 15 * h]
        yr[v, edge] = e
        yr[v, edge + 1] = e
    again = [
        remote(yr.at[:, pl.ds(2 + low, 2)], yr.at[:, pl.ds(edge, 2)], 11, mate),
        remote(yt.at[:, pl.ds(8, 2)], yt.at[:, pl.ds(0, 2)], 12, right),
        remote(yt.at[:, pl.ds(2, 2)], yt.at[:, pl.ds(10, 2)], 13, left),
    ]

    landed(ab.at[pl.ds(0, 15)], 10)
    lane8 = lax.broadcasted_iota(jnp.int32, (16, LAT), 1)
    pick = jnp.where(lane8 == s, 1.0, 0.0).astype(BF16)
    mine_hi, mine_lo = split2(ab[pl.ds(8 * h, 8)].reshape(LAT, LAT))
    currents = (nt(pick, mine_hi) + nt(pick, mine_lo))[:8]

    def apply_block(vector):
        hi, lo = split2(vector)
        both = nt(jnp.concatenate([hi, lo], axis=0), inv_hi)
        return both[:8] + both[8:] + nt(jnp.concatenate([hi, lo], axis=0), inv_lo)[:8]

    lane_1 = lax.broadcasted_iota(jnp.int32, (8, LAT), 1)
    col_first, col_last = lane_1 == 0, lane_1 == LAT - 1
    keep_n = jnp.where(s > 0, 1.0, 0.0).astype(F32)
    keep_s = jnp.where(s < NZ * NXY - 1, 1.0, 0.0).astype(F32)
    keep_w = h.astype(F32)
    keep_e = (1 - h).astype(F32)

    potential = apply_block(currents)
    hops = []
    for k in range(SWEEPS - 1):
        prow[k] = potential[:1]
        trio = [
            remote(prow.at[k], sweep.at[3 * k], 14 + 3 * k, right),
            remote(prow.at[k], sweep.at[3 * k + 1], 15 + 3 * k, left),
            remote(prow.at[k], sweep.at[3 * k + 2], 16 + 3 * k, mate),
        ]
        hops += trio
        if k == 0:
            lat_pass(yr, 2, acc)
        if k == 1:
            for c in again:
                c.wait_recv()
            radial_pass(yr, acc)
        for c in trio:
            c.wait_recv()
        north = jnp.broadcast_to(sweep[3 * k], (8, LAT)) * keep_n
        south = jnp.broadcast_to(sweep[3 * k + 1], (8, LAT)) * keep_s
        other = jnp.broadcast_to(sweep[3 * k + 2], (8, LAT))
        west = jnp.where(col_first, pltpu.roll(other, 1, 1) * keep_w, pltpu.roll(potential, 1, 1))
        east = jnp.where(col_last, pltpu.roll(other, LAT - 1, 1) * keep_e, pltpu.roll(potential, LAT - 1, 1))
        coupled = currents + cond[0] * north + cond[1] * south + cond[2] * west + cond[3] * east
        potential = apply_block(coupled)

    out_pot[...] = potential[:1]
    prow[SWEEPS - 1] = potential[:1]
    zp[slot] = potential[:1]
    for device in line:
        remote(prow.at[SWEEPS - 1], zp.at[slot], 23, device)

    lon_pass(yt, acct)

    landed(zp.at[pl.ds(0, 15)], 23)
    ps[...] = jnp.concatenate(
        [jnp.concatenate([zp[2 * k], zp[2 * k + 1]], axis=1) for k in range(NZ)], axis=0
    )
    ap[xy] = ps[...]
    for device in plane:
        remote(ps, ap.at[xy], 24, device)

    def last_step(l, carry):
        for v in range(8):
            out_state[v, l] = 0.5 * (
                state[v, l] + yr[v, l + 2] - (0.5 * TIME_STEP) * (acc[v, l] + acct[v, :, l, :])
            )
        return carry

    lax.fori_loop(0, R, last_step, 0)

    landed(ap.at[pl.ds(0, 15)], 24)
    lane256 = lax.broadcasted_iota(jnp.int32, (16, 2 * LAT), 1)
    sub256 = lax.broadcasted_iota(jnp.int32, (16, 2 * LAT), 0)
    pick2 = jnp.where(lane256 == 2 * s + sub256, 1.0, 0.0).astype(BF16)
    hi, lo = split2(ap[...].reshape(LAT, 2 * LAT))
    table = nt(pick2, hi) + nt(pick2, lo)
    tab0 = jnp.broadcast_to(table[0:1], (LON, LAT))
    tab1 = jnp.broadcast_to(table[1:2], (LON, LAT))

    def gather_step(l, carry):
        node = foot[l]
        row = jnp.right_shift(node, 8)
        even = jnp.bitwise_and(node, 1) == 0
        out_foot[l] = jnp.where(
            even,
            jnp.take_along_axis(tab0, row, axis=1, mode="promise_in_bounds"),
            jnp.take_along_axis(tab1, row, axis=1, mode="promise_in_bounds"),
        )
        return carry

    lax.fori_loop(0, R, gather_step, 0)

    for c in copies + again + hops:
        c.wait_send()
    sent(zb.at[pl.ds(0, 15)], 9)
    sent(ab.at[pl.ds(0, 15)], 10)
    sent(zp.at[pl.ds(0, 15)], 23)
    sent(ap.at[pl.ds(0, 15)], 24)


def body(state, footpoints, conductance, inverse_blocks):
    vmem = pl.BlockSpec(memory_space=pltpu.VMEM)
    return pl.pallas_call(
        kernel,
        out_shape=(
            jax.ShapeDtypeStruct((8, R, LON, LAT), F32),
            jax.ShapeDtypeStruct((1, LAT), F32),
            jax.ShapeDtypeStruct((R, LON, LAT), F32),
        ),
        in_specs=[vmem] * 4,
        out_specs=(vmem, vmem, vmem),
        scratch_shapes=[
            pltpu.VMEM((8, R + 4, LON, LAT), F32),
            pltpu.VMEM((8, LON + 4, R, LAT), F32),
            pltpu.VMEM((8, R + 4, LON, LAT), F32),
            pltpu.VMEM((8, LON + 4, R, LAT), F32),
            pltpu.VMEM((8, R, LON, LAT), F32),
            pltpu.VMEM((8, LON, R, LAT), F32),
            pltpu.VMEM((2, LON, R, LAT), F32),
            pltpu.VMEM((2, LAT), F32),
            pltpu.VMEM((16, 2, LAT), F32),
            pltpu.VMEM((16, LAT), F32),
            pltpu.VMEM((NXY, 16, LAT), F32),
            pltpu.VMEM((SWEEPS, 1, LAT), F32),
            pltpu.VMEM((9, 1, LAT), F32),
            pltpu.VMEM((16, 1, LAT), F32),
            pltpu.VMEM((NZ, 2 * LAT), F32),
            pltpu.VMEM((NXY, NZ, 2 * LAT), F32),
            pltpu.SemaphoreType.DMA((25,)),
            pltpu.SemaphoreType.DMA((25,)),
        ],
        compiler_params=pltpu.CompilerParams(
            collective_id=0, has_side_effects=True, vmem_limit_bytes=40 << 20
        ),
    )(state, footpoints, conductance, inverse_blocks)


def solution(mesh):
    return jax.shard_map(
        body,
        mesh=mesh,
        in_specs=(
            P(None, "radial", "shell", None),
            P("radial", "shell", None),
            P(None, "shell", "radial"),
            P("shell", "radial", None, None),
        ),
        out_specs=(
            P(None, "radial", "shell", None),
            P("shell", "radial"),
            P("radial", "shell", None),
        ),
        check_vma=False,
    )
```

time: 685 us -> 61 us (0.09)
  waiting for transfers between devices: 233 us -> 0 us
  local copies, waits for them, and re-layouts: 191 us -> 5.33 us
  other arithmetic: 131 us -> 0 us
  blocking collectives: 61.8 us -> 0 us
  Pallas kernels: 0 us -> 54.8 us
  starting transfers between devices: 51.8 us -> 0 us
  between operations: 15.3 us -> 0.65 us
    unnamed x2 -> x0, waiting for transfers between devices: 228 us -> none
    gather x1 -> x0, local copies, waits for them, and re-layouts: 161 us -> none  [body(): footpoint_potential = whole_table[node_slot]]
    scatter-add x1 -> x0, other arithmetic: 86.8 us -> none  [body(): jax.ops.segment_sum(cell_current, node_slot.reshape(-1), num_segments=NLA...]
    all_gather x1 -> x0, blocking collectives: 61.8 us -> none  [body(): lax.all_gather(potential.reshape(-1), ('shell', 'radial'), axis=0, tiled=...]
    pallas_call x0 -> x1, Pallas kernels: none -> 54.8 us  [body(): pl.pallas_call(kernel, out_shape=(jax.ShapeDtypeStruct((8, R, LON, LAT),...]
    ppermute x20 -> x0, starting transfers between devices: 51.8 us -> none  [the longest x10 28.9 us: padded_2(): lax.ppermute(lax.slice_in_dim(block, 0, width, axis=dim), axis, backward)]
    slice x18 -> x0, local copies, waits for them, and re-layouts: 16.1 us -> none  [the longest x6 13.6 us: pad_latitude(): return jnp.pad(field, ((0, 0), (0, 0), (0, 0), (2, 2)), mode='edge')]
    reduce_sum x12 -> x0, other arithmetic: 12.4 us -> none  [physical_flux(): field_sq = jnp.sum(magnetic * magnetic, axis=0)]
  transfers between devices with their start and end apart: 21 -> 0, of which waited for: 9 -> 0; matrix products, arithmetic and copies ran while one was open for 26% -> 0% of each run, Pallas kernels for 0% -> 0%
where the time goes in v1:
time: 61 us; the launch traced here: 60.8 us
  Pallas kernels  54.8 us (90%)
  local copies, waits for them, and re-layouts  5.33 us (9%)
  between operations  0.65 us (1%)
    pallas_call x1, Pallas kernels, body(): pl.pallas_call(kernel, out_shape=(jax.ShapeDtypeStruct((8, R, LON, LAT),...  54.8 us
    unnamed x11, local copies, waits for them, and re-layouts  5.33 us

profile of v1, /device:TPU:1, one launch (start us, length us, event | category | flops | bytes accessed | tf_op | source)
XLA Modules:
  0.0 60.8 jit_solution(12675399072628896286)
XLA Ops:
  0.6 0.0 copy-start
  0.6 1.0 %copy-done = f32[8,16,8,128]{3,2,1,0:T(8,128)S(1)} copy-done((f32[8,16,8,128]{3,2,1,0:T(8,128)S(1)}, f32[8,16,8,128]{3,2,1,0:T(8,128)}, u32[]{:S(2)}) %copy-start) | copy-done | bytes 524312
  1.7 0.0 copy-start.1
  1.7 0.8 %copy-done.1 = s32[16,8,128]{2,1,0:T(8,128)S(1)} copy-done((s32[16,8,128]{2,1,0:T(8,128)S(1)}, s32[16,8,128]{2,1,0:T(8,128)}, u32[]{:S(2)}) %copy-start.1) | copy-done | bytes 65560
  2.5 0.0 copy-start.2
  2.5 0.8 %copy-done.2 = f32[1,1,128,128]{3,2,1,0:T(8,128)S(1)} copy-done((f32[1,1,128,128]{3,2,1,0:T(8,128)S(1)}, f32[1,1,128,128]{3,2,1,0:T(8,128)}, u32[]{:S(2)}) %copy-start.2) | copy-done | bytes 65560
  3.4 0.0 copy-start.3
  3.4 0.7 %copy-done.3 = f32[4,1,128]{2,1,0:T(1,128)S(1)} copy-done((f32[4,1,128]{2,1,0:T(1,128)S(1)}, f32[4,1,128]{2,1,0:T(1,128)}, u32[]{:S(2)}) %copy-start.3) | copy-done | bytes 2072
  4.0 54.8 %shard_map.67 = (f32[8,16,8,128]{3,2,1,0:T(8,128)S(1)}, f32[1,128]{1,0:T(1,128)S(1)}, f32[16,8,128]{2,1,0:T(8,128)S(1)}) custom-call(f32[8,16,8,128]{3,2,1,0:T(8,128)S(1)} %copy-done, s32[16,8,128]{2,1,0:T(8,128)S(1)} %copy-done.1, f32[4,1,128]{2,1,0:T(1,128)S(1)} %copy-done.3, f32[1,1,128,128]{3,2,1,0:T(8,128)S(1)} %copy-done.2), custom_call_target="tpu_custom_call" | custom-call | tf_op jit(solution)/shard_map/pallas_call | solution.py:419
  58.8 0.8 %copy.10 = f32[8,16,8,128]{3,2,1,0:T(8,128)} copy(f32[8,16,8,128]{3,2,1,0:T(8,128)S(1)} %get-tuple-element.6) | data formatting | bytes 1048576
  59.6 0.5 copy.11
  60.1 0.6 %copy.12 = f32[16,8,128]{2,1,0:T(8,128)} copy(f32[16,8,128]{2,1,0:T(8,128)S(1)} %get-tuple-element.8) | data formatting | bytes 131072
Async XLA Ops:
  0.6 1.0 %copy-start = (f32[8,16,8,128]{3,2,1,0:T(8,128)S(1)}, f32[8,16,8,128]{3,2,1,0:T(8,128)}, u32[]{:S(2)}) copy-start(f32[8,16,8,128]{3,2,1,0:T(8,128)} %state.1) | copy-start | bytes 1572868
  1.7 0.8 %copy-start.1 = (s32[16,8,128]{2,1,0:T(8,128)S(1)}, s32[16,8,128]{2,1,0:T(8,128)}, u32[]{:S(2)}) copy-start(s32[16,8,128]{2,1,0:T(8,128)} %foot.1) | copy-start | bytes 196612
  2.5 0.8 %copy-start.2 = (f32[1,1,128,128]{3,2,1,0:T(8,128)S(1)}, f32[1,1,128,128]{3,2,1,0:T(8,128)}, u32[]{:S(2)}) copy-start(f32[1,1,128,128]{3,2,1,0:T(8,128)} %inv.1) | copy-start | bytes 196612
  3.4 0.7 %copy-start.3 = (f32[4,1,128]{2,1,0:T(1,128)S(1)}, f32[4,1,128]{2,1,0:T(1,128)}, u32[]{:S(2)}) copy-start(f32[4,1,128]{2,1,0:T(1,128)} %cond.1) | copy-start | bytes 6148

commit v2 on v1

v2 whole, which is shorter than its diff:
```python
import jax
import jax.numpy as jnp
from jax import lax
from jax.experimental import pallas as pl
from jax.experimental.pallas import tpu as pltpu
from jax.sharding import PartitionSpec as P

F32 = jnp.float32
BF16 = jnp.bfloat16
GAMMA = 5.0 / 3.0
TIME_STEP = 0.02
CELL_AREA = 0.125
REACH = 3

NZ = 8
NXY = 16
R = 16
LON = 8
LAT = 128
FAR_FIRST_Z = (4, 3, 5, 2, 6, 1, 7)
FAR_FIRST_XY = (10, 6, 14, 2, 9, 11, 5, 7, 13, 15, 1, 3, 8, 4, 12)

NT = (((1,), (1,)), ((), ()))
MESH = pl.DeviceIdType.MESH


def minmod(a, b):
    return jnp.maximum(jnp.minimum(a, jnp.maximum(b, 0.0)), jnp.minimum(b, 0.0))


def flux(u, d):
    density, energy = u[0], u[7]
    inv = 1.0 / density
    vel = [u[1] * inv, u[2] * inv, u[3] * inv]
    mag = u[4:7]
    field_sq = mag[0] * mag[0] + mag[1] * mag[1] + mag[2] * mag[2]
    kinetic = vel[0] * vel[0] + vel[1] * vel[1] + vel[2] * vel[2]
    half_sq = 0.5 * field_sq
    pressure = (GAMMA - 1.0) * (energy - 0.5 * density * kinetic - half_sq)
    total = pressure + half_sq
    vn, bn = vel[d], mag[d]
    align = vel[0] * mag[0] + vel[1] * mag[1] + vel[2] * mag[2]
    out = [u[1 + d]]
    for k in range(3):
        m = u[1 + k] * vn - mag[k] * bn
        out.append(m + total if k == d else m)
    for k in range(3):
        out.append(None if k == d else vn * mag[k] - bn * vel[k])
    out.append((energy + total) * vn - bn * align)
    signal = jnp.abs(vn) + jnp.sqrt((GAMMA * jnp.abs(pressure) + field_sq) * inv)
    return out, signal


def face(left, right, d):
    fl, sl = flux(left, d)
    fr, sr = flux(right, d)
    top = jnp.maximum(sl, sr)
    out = []
    for k in range(8):
        jump = top * (right[k] - left[k])
        out.append(-jump if fl[k] is None else (fl[k] + fr[k]) - jump)
    return out


def split2(x):
    hi = x.astype(BF16)
    lo = (x - hi.astype(F32)).astype(BF16)
    return hi, lo


def nt(a, b):
    return lax.dot_general(a, b, NT, preferred_element_type=F32)


def lat_pass(src, base, acc):
    lane = lax.broadcasted_iota(jnp.int32, (2, LON, LAT), 2)
    last, first = lane == LAT - 1, lane == 0

    def step(i, carry):
        l = i * 2
        left, right = [], []
        for v in range(8):
            u = src[v, pl.ds(base + l, 2)]
            d = jnp.where(last, 0.0, pltpu.roll(u, LAT - 1, 2) - u)
            h = 0.5 * minmod(d, pltpu.roll(d, 1, 2))
            left.append(u + h)
            r = u - h
            right.append(jnp.where(last, r, pltpu.roll(r, LAT - 1, 2)))
        fl, sl = flux(left, 2)
        fr, sr = flux(right, 2)
        top = jnp.maximum(sl, sr)
        for v in range(8):
            jump = top * (right[v] - left[v])
            if fl[v] is None:
                f = -jump
                acc[v, pl.ds(l, 2)] = f - jnp.where(first, 0.0, pltpu.roll(f, 1, 2))
            else:
                f = (fl[v] + fr[v]) - jump
                acc[v, pl.ds(l, 2)] = f - jnp.where(first, 2.0 * fl[v], pltpu.roll(f, 1, 2))
        return carry

    lax.fori_loop(0, R // 2, step, 0)


def radial_pass(ext, acc):
    half = R // 2

    def cells(i):
        return [jnp.stack([ext[v, i], ext[v, i + half]]) for v in range(8)]

    def advance(f, prev, here):
        nxt = cells(f + 2)
        left, right, jumps = [], [], []
        for v in range(8):
            d = nxt[v] - here[v]
            h = 0.5 * minmod(d, prev[v])
            jumps.append(d)
            left.append(here[v] + h)
            right.append(here[v] - h)
        return nxt, jumps, left, right

    c0, c1 = cells(0), cells(1)
    prev = [c1[v] - c0[v] for v in range(8)]
    here, prev, left, _ = advance(0, prev, c1)
    here, prev, left2, right = advance(1, prev, here)
    f0 = face(left, right, 0)

    def step(i, carry):
        here, prev, left, f0 = carry
        here, prev, left2, right = advance(i + 2, prev, here)
        f1 = face(left, right, 0)
        for v in range(8):
            df = f1[v] - f0[v]
            acc[v, i] += df[0]
            acc[v, i + half] += df[1]
        return here, prev, left2, f1

    lax.fori_loop(0, half, step, (here, prev, left2, f0))


def lon_pass(ext, acc):
    def advance(i, prev, here):
        left, right, jumps, nxt = [], [], [], []
        for v in range(8):
            n = ext[v, i]
            d = n - here[v]
            h = 0.5 * minmod(d, prev[v])
            nxt.append(n)
            jumps.append(d)
            left.append(here[v] + h)
            right.append(here[v] - h)
        return nxt, jumps, left, right

    c0 = [ext[v, 0] for v in range(8)]
    c1 = [ext[v, 1] for v in range(8)]
    prev = [c1[v] - c0[v] for v in range(8)]
    here, prev, left, _ = advance(2, prev, c1)
    here, prev, left2, right = advance(3, prev, here)
    f0 = face(left, right, 1)

    def step(i, carry):
        here, prev, left, f0 = carry
        here, prev, left2, right = advance(i + 4, prev, here)
        f1 = face(left, right, 1)
        for v in range(8):
            acc[v, i] = f1[v] - f0[v]
        return here, prev, left2, f1

    lax.fori_loop(0, LON, step, (here, prev, left2, f0))


def kernel(
    state, foot_hbm, cond, inv,
    out_state, out_pot, out_table,
    foot, xr, xt, yr, yt, acc, acct, dt1, edge_in,
    part, zb, a1s, a1, prow, zp, a2s, a2,
    blocks, conds, qa, qb, green, kk,
    send_sem, recv_sem, local_sem,
):
    s = lax.axis_index("shell")
    h = lax.axis_index("radial")
    ring = NZ * NXY
    z, xy = s % NZ, s // NZ
    base = s - z
    right = ((s + 1) % ring, h)
    left = ((s + ring - 1) % ring, h)
    mate = (s, 1 - h)
    line = [(base + (z + k) % NZ, c) for k in FAR_FIRST_Z for c in (0, 1)] + [mate]
    plane = [((xy + k) % NXY, ((xy + k) % NXY * NZ + z, h)) for k in FAR_FIRST_XY]
    slot = z * 2 + h
    count = [0]

    def fresh():
        count[0] += 1
        return count[0] - 1

    def remote(src, dst, device, n=None):
        n = fresh() if n is None else n
        copy = pltpu.make_async_remote_copy(
            src_ref=src, dst_ref=dst, send_sem=send_sem.at[n], recv_sem=recv_sem.at[n],
            device_id=device, device_id_type=MESH,
        )
        copy.start()
        return copy

    def landed(ref, n):
        pltpu.make_async_copy(ref, ref, recv_sem.at[n]).wait()

    def sent(ref, n):
        pltpu.make_async_copy(ref, ref, send_sem.at[n]).wait()

    barrier = pltpu.get_barrier_semaphore()
    partners = line + [p for _, p in plane] + [right, left]
    for device in partners:
        pl.semaphore_signal(barrier, inc=1, device_id=device, device_id_type=MESH)

    inner = pl.ds(2, R)
    loads = [
        pltpu.make_async_copy(state.at[pl.ds(4, 3)], xr.at[pl.ds(4, 3), inner], local_sem.at[0]),
        pltpu.make_async_copy(state.at[pl.ds(0, 4)], xr.at[pl.ds(0, 4), inner], local_sem.at[1]),
        pltpu.make_async_copy(state.at[pl.ds(7, 1)], xr.at[pl.ds(7, 1), inner], local_sem.at[2]),
        pltpu.make_async_copy(foot_hbm, foot, local_sem.at[3]),
        pltpu.make_async_copy(inv.at[0, 0], blocks.at[3, 0], local_sem.at[4]),
        pltpu.make_async_copy(cond, conds.at[3, 0], local_sem.at[5]),
    ]
    for c in loads:
        c.start()

    def turn(dst, src, v):
        for j in range(LON):
            dst[v, j + 2] = src[v, 2 : R + 2, j, :]

    loads[0].wait()
    for v in (4, 6):
        turn(xt, xr, v)
    pl.semaphore_wait(barrier, len(partners))

    edge, low = 18 * h, 14 * (1 - h)
    copies, near = [], []
    for k, v in enumerate((6, 4)):
        near.append(remote(xt.at[v, 9], edge_in.at[k, 0], right))
        near.append(remote(xt.at[v, 2], edge_in.at[k, 1], left))
    near.append(remote(state.at[pl.ds(4, 3), pl.ds(low, 2)], xr.at[pl.ds(4, 3), pl.ds(edge, 2)], mate))

    own_block, own_cond = inv.at[0, 0], cond
    go_right = [remote(own_cond, conds.at[2, 0], right), remote(own_block, blocks.at[2, 0], right)]
    go_left = [remote(own_cond, conds.at[4, 0], left), remote(own_block, blocks.at[4, 0], left)]
    go_mate = [remote(own_cond, conds.at[3, 1], mate), remote(own_block, blocks.at[3, 1], mate)]
    side = [
        remote(state.at[pl.ds(0, 4), pl.ds(low, 2)], xr.at[pl.ds(0, 4), pl.ds(edge, 2)], mate),
        remote(state.at[pl.ds(7, 1), pl.ds(low, 2)], xr.at[pl.ds(7, 1), pl.ds(edge, 2)], mate),
    ]

    loads[1].wait()
    loads[2].wait()
    for v in (5, 0, 1, 2, 3, 7):
        turn(xt, xr, v)
    for v in range(8):
        e = xr[v, 2 + 15 * h]
        xr[v, edge] = e
        xr[v, edge + 1] = e
    lat_pass(xr, 2, acc)

    loads[3].wait()
    for c in near:
        c.wait_recv()
    for k, v in enumerate((6, 4)):
        dt1[k, 0] = xt[v, 3] - edge_in[k, 0]
        for j in range(1, LON - 1):
            dt1[k, j] = xt[v, j + 3] - xt[v, j + 1]
        dt1[k, LON - 1] = edge_in[k, 1] - xt[v, LON]
    lane = lax.broadcasted_iota(jnp.int32, (LON, LAT), 1)
    first, last = lane == 0, lane == LAT - 1
    row16 = lax.broadcasted_iota(jnp.int32, (16, LAT), 0)
    lane16 = lax.broadcasted_iota(jnp.int32, (16, LAT), 1)

    def along_lat(b):
        up = jnp.where(last, b, pltpu.roll(b, LAT - 1, 1))
        down = jnp.where(first, b, pltpu.roll(b, 1, 1))
        return up - down

    def current_step(i, total):
        a, ones = [], []
        for t in range(4):
            l = i * 4 + t
            b = [xr[v, l + 2] for v in (4, 5, 6)]
            up = [xr[v, l + 3] for v in (5, 6)]
            dn = [xr[v, l + 1] for v in (5, 6)]
            c0 = dt1[0, :, l, :] - along_lat(b[1])
            c1 = along_lat(b[0]) - (up[1] - dn[1])
            c2 = (up[0] - dn[0]) - dt1[1, :, l, :]
            sq = b[0] * b[0] + b[1] * b[1] + b[2] * b[2]
            val = (0.5 * CELL_AREA) * (c0 * b[0] + c1 * b[1] + c2 * b[2]) / jnp.sqrt(1.0 + sq)
            hi = val.astype(BF16).astype(F32)
            lo = val - hi
            node = foot[l]
            row = jnp.right_shift(node, 8)
            group = jnp.bitwise_and(node, 1) * 8 + jnp.right_shift(row, 4)
            within = jnp.bitwise_and(row, 15)
            for j in range(LON):
                hit = jnp.broadcast_to(group[j : j + 1], (16, LAT)) == row16
                top = jnp.where(hit, jnp.broadcast_to(hi[j : j + 1], (16, LAT)), 0.0)
                low_part = jnp.where(hit, jnp.broadcast_to(lo[j : j + 1], (16, LAT)), 0.0)
                a.append(jnp.concatenate([top.astype(BF16), low_part.astype(BF16)], axis=0))
                one = jnp.where(jnp.broadcast_to(within[j : j + 1], (16, LAT)) == row16, 1.0, 0.0)
                ones.append(one.astype(BF16))
        return total + nt(jnp.concatenate(a, axis=1), jnp.concatenate(ones, axis=1))

    total = lax.fori_loop(0, R // 4, current_step, jnp.zeros((32, 16), F32))
    spread = jnp.where(jnp.bitwise_and(lane16, 15) == row16, 1.0, 0.0).astype(BF16)
    t_hi, t_lo = split2(total[:16] + total[16:])
    total = jnp.dot(jnp.concatenate([t_hi, t_lo], axis=0), spread, preferred_element_type=F32)
    total = jnp.where(
        jnp.right_shift(lane16, 4) == jnp.bitwise_and(row16, 7), total[:16] + total[16:], 0.0
    )
    mine = jnp.concatenate(
        [jnp.sum(total[:8], axis=0, keepdims=True), jnp.sum(total[8:], axis=0, keepdims=True)], axis=0
    )
    part[...] = mine
    zb[slot] = mine
    n_zb = fresh()
    for device in line:
        remote(part, zb.at[slot], device, n_zb)

    copies += [
        remote(xt.at[:, pl.ds(8, 2)], xt.at[:, pl.ds(0, 2)], right),
        remote(xt.at[:, pl.ds(2, 2)], xt.at[:, pl.ds(10, 2)], left),
    ]
    for c in go_right + go_left + go_mate + side:
        c.wait_recv()
    hop_right = [remote(conds.at[2, 0], conds.at[1, 0], right), remote(blocks.at[2, 0], blocks.at[1, 0], right)]
    hop_left = [remote(conds.at[4, 0], conds.at[5, 0], left), remote(blocks.at[4, 0], blocks.at[5, 0], left)]
    hop_mate = [
        remote(conds.at[2, 0], conds.at[2, 1], mate), remote(blocks.at[2, 0], blocks.at[2, 1], mate),
        remote(conds.at[4, 0], conds.at[4, 1], mate), remote(blocks.at[4, 0], blocks.at[4, 1], mate),
    ]
    loads[4].wait()
    loads[5].wait()

    lane32 = lax.broadcasted_iota(jnp.int32, (32, LAT), 1)
    low32, high32 = lane32 == 0, lane32 == LAT - 1
    is_low = ((1 - h).astype(F32), h.astype(F32))
    is_high = (h.astype(F32), (1 - h).astype(F32))

    def north(d, c):
        return conds[d + 3, c, 0] * jnp.where(s + d == 0, 0.0, 1.0)

    def south(d, c):
        return conds[d + 3, c, 1] * jnp.where(s + d == ring - 1, 0.0, 1.0)

    def widen(source, target, level):
        there = lambda d, c: abs(d) <= level - c
        for c in (0, 1):
            for d in range(c - level - 1, level + 2 - c):
                for i in range(0, LAT, 32):
                    rows = pl.ds(i, 32)
                    terms = []
                    if there(d + 1, c):
                        terms.append(source(d + 1, c)[rows] * north(d + 1, c))
                    if there(d - 1, c):
                        terms.append(source(d - 1, c)[rows] * south(d - 1, c))
                    w, e = None, None
                    if there(d, c):
                        me = source(d, c)[rows]
                        w, e = me * conds[d + 3, c, 2], me * conds[d + 3, c, 3]
                    if there(d, 1 - c):
                        ot = source(d, 1 - c)[rows]
                        zero = jnp.zeros_like(ot)
                        w = jnp.where(low32, ot * (conds[d + 3, 1 - c, 2] * is_low[c]), zero if w is None else w)
                        e = jnp.where(high32, ot * (conds[d + 3, 1 - c, 3] * is_high[c]), zero if e is None else e)
                    elif w is not None:
                        w, e = jnp.where(low32, 0.0, w), jnp.where(high32, 0.0, e)
                    if w is not None:
                        terms += [pltpu.roll(w, LAT - 1, 1), pltpu.roll(e, 1, 1)]
                    k_hi, k_lo = split2(sum(terms[1:], terms[0]))
                    kk[rows, :] = jnp.concatenate([k_hi, k_hi, k_lo], axis=1)
                b_hi, b_lo = split2(blocks[d + 3, c])
                q = jnp.dot(kk[...], jnp.concatenate([b_hi, b_lo, b_hi], axis=0), preferred_element_type=F32)
                if target is not None:
                    target[d + 3, c] = q
                if there(d, c):
                    green[d + 3, c] += q
                else:
                    green[d + 3, c] = q

    green[3, 0] = blocks[3, 0]
    widen(lambda d, c: blocks.at[d + 3, c], qb, 0)
    radial_pass(xr, acc)

    landed(zb.at[pl.ds(0, 15)], n_zb)
    columns = jnp.concatenate([zb[2 * k] + zb[2 * k + 1] for k in range(NZ)], axis=0)
    row128 = lax.broadcasted_iota(jnp.int32, (LAT, LAT), 0)
    lane128 = lax.broadcasted_iota(jnp.int32, (LAT, LAT), 1)
    placed = jnp.where(
        jnp.right_shift(row128, 4) == xy % 8, jnp.concatenate([columns] * 8, axis=0), 0.0
    )
    pick = jnp.where(lane128 == row128 + (z - REACH), 1.0, 0.0).astype(BF16)
    p_hi, p_lo = split2(placed)
    a1s[...] = (nt(pick, p_hi) + nt(pick, p_lo)).reshape(NXY, 8, LAT)
    n_a1 = fresh()
    for to, device in plane:
        remote(a1s.at[to], a1.at[xy], device, n_a1)
    a1[xy] = a1s[xy]

    for c in hop_right + hop_left + hop_mate:
        c.wait_recv()
    end_right = [remote(blocks.at[1, 0], blocks.at[0, 0], right)]
    end_left = [remote(blocks.at[5, 0], blocks.at[6, 0], left)]
    end_mate = [remote(blocks.at[1, 0], blocks.at[1, 1], mate), remote(blocks.at[5, 0], blocks.at[5, 1], mate)]
    widen(lambda d, c: qb.at[d + 3, c], qa, 1)
    for c in copies:
        c.wait_recv()
    lon_pass(xt, acct)

    def section_one(l, carry):
        for v in range(8):
            yr[v, l + 2] = xr[v, l + 2] - (0.5 * TIME_STEP) * (acc[v, l] + acct[v, :, l, :])
        return carry

    lax.fori_loop(0, R, section_one, 0)
    for v in range(8):
        turn(yt, yr, v)
        e = yr[v, 2 + 15 * h]
        yr[v, edge] = e
        yr[v, edge + 1] = e
    for c in end_right + end_left + end_mate:
        c.wait_recv()
    widen(lambda d, c: qa.at[d + 3, c], None, 2)

    landed(a1.at[pl.ds(0, 15)], n_a1)
    out = jnp.zeros((LAT, LAT), F32)
    for c in (0, 1):
        first_source = 8 * h if c == 0 else 8 * (1 - h)
        rows = a1[first_source]
        for k in range(1, 8):
            rows = rows + a1[first_source + k]
        for d in range(c - REACH, REACH + 1 - c):
            out = out + green[d + 3, c] * jnp.broadcast_to(rows[d + 3 : d + 4], (LAT, LAT))
    o_hi, o_lo = split2(out)
    all_ones = jnp.ones((16, LAT), BF16)
    potential = (nt(all_ones, o_hi) + nt(all_ones, o_lo))[:1]
    out_pot[...] = potential
    prow[...] = potential
    zp[slot] = potential
    n_zp = fresh()
    for device in line:
        remote(prow, zp.at[slot], device, n_zp)

    again = [
        remote(yr.at[:, pl.ds(2 + low, 2)], yr.at[:, pl.ds(edge, 2)], mate),
        remote(yt.at[:, pl.ds(8, 2)], yt.at[:, pl.ds(0, 2)], right),
        remote(yt.at[:, pl.ds(2, 2)], yt.at[:, pl.ds(10, 2)], left),
    ]
    lat_pass(yr, 2, acc)

    landed(zp.at[pl.ds(0, 15)], n_zp)
    lines = jnp.concatenate(
        [jnp.concatenate([zp[2 * k], zp[2 * k + 1]], axis=1) for k in range(NZ)], axis=0
    )
    row256 = lax.broadcasted_iota(jnp.int32, (LAT, 2 * LAT), 0)
    placed = jnp.where(jnp.right_shift(row256, 3) == xy, jnp.concatenate([lines] * NXY, axis=0), 0.0)
    m = lax.broadcasted_iota(jnp.int32, (2 * NXY, 2 * LAT), 0)
    n = lax.broadcasted_iota(jnp.int32, (2 * NXY, 2 * LAT), 1)
    pick2 = jnp.where(
        n == 2 * (jnp.right_shift(m, 1) * NZ + z) + jnp.bitwise_and(m, 1), 1.0, 0.0
    ).astype(BF16)
    l_hi, l_lo = split2(placed)
    picked = nt(pick2, l_hi) + nt(pick2, l_lo)
    for k in range(NXY):
        a2s[k] = picked[2 * k : 2 * k + 2]
    n_a2 = fresh()
    for to, device in plane:
        remote(a2s.at[to], a2.at[xy], device, n_a2)
    a2[xy] = a2s[xy]

    for c in again:
        c.wait_recv()
    radial_pass(yr, acc)
    lon_pass(yt, acct)

    def last_step(l, carry):
        for v in range(8):
            out_state[v, l] = 0.5 * (
                xr[v, l + 2] + yr[v, l + 2] - (0.5 * TIME_STEP) * (acc[v, l] + acct[v, :, l, :])
            )
        return carry

    lax.fori_loop(0, R, last_step, 0)

    landed(a2.at[pl.ds(0, 15)], n_a2)
    table = a2[0]
    for k in range(1, NXY):
        table = table + a2[k]
    out_table[...] = table

    for c in (
        near + copies + side + again + go_right + go_left + go_mate + hop_right + hop_left + hop_mate
        + end_right + end_left + end_mate
    ):
        c.wait_send()
    sent(zb.at[pl.ds(0, 15)], n_zb)
    sent(a1.at[pl.ds(0, 15)], n_a1)
    sent(zp.at[pl.ds(0, 15)], n_zp)
    sent(a2.at[pl.ds(0, 15)], n_a2)
    assert count[0] <= N_SEMS, count[0]


def finish(state, pot, table, foot, out_state, out_pot, out_foot, buf, sem):
    copies = [
        pltpu.make_async_copy(state, out_state, sem.at[0]),
        pltpu.make_async_copy(pot, out_pot, sem.at[1]),
    ]
    for c in copies:
        c.start()
    tab0 = jnp.broadcast_to(table[0:1, :], (LON, LAT))
    tab1 = jnp.broadcast_to(table[1:2, :], (LON, LAT))
    for l in range(R):
        node = foot[l]
        row = jnp.right_shift(node, 8)
        buf[l] = jnp.where(
            jnp.bitwise_and(node, 1) == 0,
            jnp.take_along_axis(tab0, row, axis=1, mode="promise_in_bounds"),
            jnp.take_along_axis(tab1, row, axis=1, mode="promise_in_bounds"),
        )
    copies.append(pltpu.make_async_copy(buf, out_foot, sem.at[2]))
    copies[2].start()
    for c in copies:
        c.wait()


N_SEMS = 48


def body(state, footpoints, conductance, inverse_blocks):
    vmem = pl.BlockSpec(memory_space=pltpu.VMEM)
    hbm = pl.BlockSpec(memory_space=pltpu.HBM)
    whole = (
        jax.ShapeDtypeStruct((8, R, LON, LAT), F32),
        jax.ShapeDtypeStruct((1, LAT), F32),
    )
    cells, potential, table = pl.pallas_call(
        kernel,
        out_shape=whole + (jax.ShapeDtypeStruct((2, LAT), F32),),
        in_specs=[hbm] * 4,
        out_specs=(vmem, vmem, vmem),
        scratch_shapes=[
            pltpu.VMEM((R, LON, LAT), jnp.int32),
            pltpu.VMEM((8, R + 4, LON, LAT), F32),
            pltpu.VMEM((8, LON + 4, R, LAT), F32),
            pltpu.VMEM((8, R + 4, LON, LAT), F32),
            pltpu.VMEM((8, LON + 4, R, LAT), F32),
            pltpu.VMEM((8, R, LON, LAT), F32),
            pltpu.VMEM((8, LON, R, LAT), F32),
            pltpu.VMEM((2, LON, R, LAT), F32),
            pltpu.VMEM((2, 2, R, LAT), F32),
            pltpu.VMEM((2, LAT), F32),
            pltpu.VMEM((16, 2, LAT), F32),
            pltpu.VMEM((NXY, 8, LAT), F32),
            pltpu.VMEM((NXY, 8, LAT), F32),
            pltpu.VMEM((1, LAT), F32),
            pltpu.VMEM((16, 1, LAT), F32),
            pltpu.VMEM((NXY, 2, LAT), F32),
            pltpu.VMEM((NXY, 2, LAT), F32),
            pltpu.VMEM((7, 2, LAT, LAT), F32),
            pltpu.VMEM((7, 2, 4, 1, LAT), F32),
            pltpu.VMEM((7, 2, LAT, LAT), F32),
            pltpu.VMEM((7, 2, LAT, LAT), F32),
            pltpu.VMEM((7, 2, LAT, LAT), F32),
            pltpu.VMEM((LAT, 3 * LAT), BF16),
            pltpu.SemaphoreType.DMA((N_SEMS,)),
            pltpu.SemaphoreType.DMA((N_SEMS,)),
            pltpu.SemaphoreType.DMA((6,)),
        ],
        compiler_params=pltpu.CompilerParams(
            collective_id=0, has_side_effects=True, vmem_limit_bytes=40 << 20
        ),
    )(state, footpoints, conductance, inverse_blocks)
    return pl.pallas_call(
        finish,
        out_shape=whole + (jax.ShapeDtypeStruct((R, LON, LAT), F32),),
        in_specs=[vmem] * 4,
        out_specs=(hbm, hbm, hbm),
        scratch_shapes=[pltpu.VMEM((R, LON, LAT), F32), pltpu.SemaphoreType.DMA((3,))],
    )(cells, potential, table, footpoints)


def solution(mesh):
    return jax.shard_map(
        body,
        mesh=mesh,
        in_specs=(
            P(None, "radial", "shell", None),
            P("radial", "shell", None),
            P(None, "shell", "radial"),
            P("shell", "radial", None, None),
        ),
        out_specs=(
            P(None, "radial", "shell", None),
            P("shell", "radial"),
            P("radial", "shell", None),
        ),
        check_vma=False,
    )
```

time: 61 us -> 49 us (0.80)
  Pallas kernels: 54.8 us -> 43.3 us
    pallas_call x1 -> x2, Pallas kernels: 54.8 us -> 43.3 us  [the longest x1 41.4 us: body(): pl.pallas_call(kernel, out_shape=whole + (jax.ShapeDtypeStruct((2, LAT),...]
    unnamed x11 -> x14, local copies, waits for them, and re-layouts: 5.33 us -> 4.74 us
where the time goes in v2:
time: 49 us; the launch traced here: 48.7 us
  Pallas kernels  43.3 us (88%)
  local copies, waits for them, and re-layouts  4.74 us (10%)
  between operations  0.66 us (1%)
    pallas_call x1, Pallas kernels, body(): pl.pallas_call(kernel, out_shape=whole + (jax.ShapeDtypeStruct((2, LAT),...  41.4 us
    unnamed x14, local copies, waits for them, and re-layouts  4.74 us
    pallas_call x1, Pallas kernels, body(): pl.pallas_call(finish, out_shape=whole + (jax.ShapeDtypeStruct((R, LON, L...  1.88 us

profile of v2, /device:TPU:1, one launch (start us, length us, event | category | flops | bytes accessed | tf_op | source)
XLA Modules:
  0.0 48.7 jit_solution(11333864114641424846)
XLA Ops:
  0.6 0.0 copy-start
  0.6 1.0 %copy-done = f32[8,16,8,128]{3,2,1,0:T(8,128)S(1)} copy-done((f32[8,16,8,128]{3,2,1,0:T(8,128)S(1)}, f32[8,16,8,128]{3,2,1,0:T(8,128)}, u32[]{:S(2)}) %copy-start) | copy-done | bytes 524312
  1.7 0.0 copy-start.2
  1.7 0.8 %copy-done.2 = s32[16,8,128]{2,1,0:T(8,128)S(1)} copy-done((s32[16,8,128]{2,1,0:T(8,128)S(1)}, s32[16,8,128]{2,1,0:T(8,128)}, u32[]{:S(2)}) %copy-start.2) | copy-done | bytes 65560
  2.5 0.0 copy-start.3
  2.5 0.8 %copy-done.3 = f32[1,1,128,128]{3,2,1,0:T(8,128)S(1)} copy-done((f32[1,1,128,128]{3,2,1,0:T(8,128)S(1)}, f32[1,1,128,128]{3,2,1,0:T(8,128)}, u32[]{:S(2)}) %copy-start.3) | copy-done | bytes 65560
  3.4 0.0 copy-start.4
  3.4 0.7 %copy-done.4 = f32[4,1,128]{2,1,0:T(1,128)S(1)} copy-done((f32[4,1,128]{2,1,0:T(1,128)S(1)}, f32[4,1,128]{2,1,0:T(1,128)}, u32[]{:S(2)}) %copy-start.4) | copy-done | bytes 2072
  4.0 41.4 %shard_map.67 = (f32[8,16,8,128]{3,2,1,0:T(8,128)S(1)}, f32[1,128]{1,0:T(1,128)S(1)}, f32[2,128]{1,0:T(2,128)S(1)}) custom-call(f32[8,16,8,128]{3,2,1,0:T(8,128)S(1)} %copy-done, s32[16,8,128]{2,1,0:T(8,128)S(1)} %copy-done.2, f32[4,1,128]{2,1,0:T(1,128)S(1)} %copy-done.4, f32[1,1,128,128]{3,2,1,0:T(8,128)S(1)} %copy-done.3), custom_call_target="tpu_custom_call" | custom-call | tf_op jit(solution)/shard_map/pallas_call | solution.py:541
  45.5 0.0 copy-start.1
  45.5 0.8 %copy-done.1 = f32[8,16,8,128]{3,2,1,0:T(8,128)} copy-done((f32[8,16,8,128]{3,2,1,0:T(8,128)}, f32[8,16,8,128]{3,2,1,0:T(8,128)S(1)}, u32[]{:S(2)}) %copy-start.1) | copy-done | bytes 524312
  46.3 0.0 copy-start.6
  46.3 0.0 copy-start.5
  46.3 0.6 %copy-done.6 = f32[1,128]{1,0:T(1,128)} copy-done((f32[1,128]{1,0:T(1,128)}, f32[1,128]{1,0:T(1,128)S(1)}, u32[]{:S(2)}) %copy-start.6) | copy-done | bytes 536
  46.8 0.0 copy-done.5
  46.8 1.9 %shard_map.68 = (f32[8,16,8,128]{3,2,1,0:T(8,128)}, f32[1,128]{1,0:T(1,128)}, f32[16,8,128]{2,1,0:T(8,128)}) custom-call(f32[8,16,8,128]{3,2,1,0:T(8,128)} %copy-done.1, f32[1,128]{1,0:T(1,128)} %copy-done.6, f32[2,128]{1,0:T(2,128)} %copy-done.5, s32[16,8,128]{2,1,0:T(8,128)} %foot.1), custom_call_target="tpu_custom_call" | custom-call | tf_op jit(solution)/shard_map/pallas_call | solution.py:578
Async XLA Ops:
  0.6 1.0 %copy-start = (f32[8,16,8,128]{3,2,1,0:T(8,128)S(1)}, f32[8,16,8,128]{3,2,1,0:T(8,128)}, u32[]{:S(2)}) copy-start(f32[8,16,8,128]{3,2,1,0:T(8,128)} %state.1) | copy-start | bytes 1572868
  1.7 0.8 %copy-start.2 = (s32[16,8,128]{2,1,0:T(8,128)S(1)}, s32[16,8,128]{2,1,0:T(8,128)}, u32[]{:S(2)}) copy-start(s32[16,8,128]{2,1,0:T(8,128)} %foot.1) | copy-start | bytes 196612
  2.5 0.8 %copy-start.3 = (f32[1,1,128,128]{3,2,1,0:T(8,128)S(1)}, f32[1,1,128,128]{3,2,1,0:T(8,128)}, u32[]{:S(2)}) copy-start(f32[1,1,128,128]{3,2,1,0:T(8,128)} %inv.1) | copy-start | bytes 196612
  3.4 0.7 %copy-start.4 = (f32[4,1,128]{2,1,0:T(1,128)S(1)}, f32[4,1,128]{2,1,0:T(1,128)}, u32[]{:S(2)}) copy-start(f32[4,1,128]{2,1,0:T(1,128)} %cond.1) | copy-start | bytes 6148
  45.5 0.8 %copy-start.1 = (f32[8,16,8,128]{3,2,1,0:T(8,128)}, f32[8,16,8,128]{3,2,1,0:T(8,128)S(1)}, u32[]{:S(2)}) copy-start(f32[8,16,8,128]{3,2,1,0:T(8,128)S(1)} %get-tuple-element.6.state) | copy-start | bytes 1572868
  46.3 0.6 %copy-start.6 = (f32[1,128]{1,0:T(1,128)}, f32[1,128]{1,0:T(1,128)S(1)}, u32[]{:S(2)}) copy-start(f32[1,128]{1,0:T(1,128)S(1)} %get-tuple-element.7.pot) | copy-start | bytes 1540
  46.3 0.6 %copy-start.5 = (f32[2,128]{1,0:T(2,128)}, f32[2,128]{1,0:T(2,128)S(1)}, u32[]{:S(2)}) copy-start(f32[2,128]{1,0:T(2,128)S(1)} %get-tuple-element.8.table) | copy-start | bytes 3076

commit v3 on v2

--- a/solution.py
+++ b/solution.py
@@ -255,6 +255,10 @@
     loads[2].wait()
     for v in (5, 0, 1, 2, 3, 7):
         turn(xt, xr, v)
+    copies += [
+        remote(xt.at[:, pl.ds(8, 2)], xt.at[:, pl.ds(0, 2)], right),
+        remote(xt.at[:, pl.ds(2, 2)], xt.at[:, pl.ds(10, 2)], left),
+    ]
     for v in range(8):
         e = xr[v, 2 + 15 * h]
         xr[v, edge] = e
@@ -322,10 +326,6 @@
     for device in line:
         remote(part, zb.at[slot], device, n_zb)
 
-    copies += [
-        remote(xt.at[:, pl.ds(8, 2)], xt.at[:, pl.ds(0, 2)], right),
-        remote(xt.at[:, pl.ds(2, 2)], xt.at[:, pl.ds(10, 2)], left),
-    ]
     for c in go_right + go_left + go_mate + side:
         c.wait_recv()
     hop_right = [remote(conds.at[2, 0], conds.at[1, 0], right), remote(blocks.at[2, 0], blocks.at[1, 0], right)]
@@ -386,6 +386,21 @@
     green[3, 0] = blocks[3, 0]
     widen(lambda d, c: blocks.at[d + 3, c], qb, 0)
     radial_pass(xr, acc)
+    for c in copies:
+        c.wait_recv()
+    lon_pass(xt, acct)
+
+    def section_one(l, carry):
+        for v in range(8):
+            yr[v, l + 2] = xr[v, l + 2] - (0.5 * TIME_STEP) * (acc[v, l] + acct[v, :, l, :])
+        return carry
+
+    lax.fori_loop(0, R, section_one, 0)
+    for v in range(8):
+        turn(yt, yr, v)
+        e = yr[v, 2 + 15 * h]
+        yr[v, edge] = e
+        yr[v, edge + 1] = e
 
     landed(zb.at[pl.ds(0, 15)], n_zb)
     columns = jnp.concatenate([zb[2 * k] + zb[2 * k + 1] for k in range(NZ)], axis=0)
@@ -407,22 +422,12 @@
     end_right = [remote(blocks.at[1, 0], blocks.at[0, 0], right)]
     end_left = [remote(blocks.at[5, 0], blocks.at[6, 0], left)]
     end_mate = [remote(blocks.at[1, 0], blocks.at[1, 1], mate), remote(blocks.at[5, 0], blocks.at[5, 1], mate)]
+    again = [
+        remote(yr.at[:, pl.ds(2 + low, 2)], yr.at[:, pl.ds(edge, 2)], mate),
+        remote(yt.at[:, pl.ds(8, 2)], yt.at[:, pl.ds(0, 2)], right),
+        remote(yt.at[:, pl.ds(2, 2)], yt.at[:, pl.ds(10, 2)], left),
+    ]
     widen(lambda d, c: qb.at[d + 3, c], qa, 1)
-    for c in copies:
-        c.wait_recv()
-    lon_pass(xt, acct)
-
-    def section_one(l, carry):
-        for v in range(8):
-            yr[v, l + 2] = xr[v, l + 2] - (0.5 * TIME_STEP) * (acc[v, l] + acct[v, :, l, :])
-        return carry
-
-    lax.fori_loop(0, R, section_one, 0)
-    for v in range(8):
-        turn(yt, yr, v)
-        e = yr[v, 2 + 15 * h]
-        yr[v, edge] = e
-        yr[v, edge + 1] = e
     for c in end_right + end_left + end_mate:
         c.wait_recv()
     widen(lambda d, c: qa.at[d + 3, c], None, 2)
@@ -446,11 +451,6 @@
     for device in line:
         remote(prow, zp.at[slot], device, n_zp)
 
-    again = [
-        remote(yr.at[:, pl.ds(2 + low, 2)], yr.at[:, pl.ds(edge, 2)], mate),
-        remote(yt.at[:, pl.ds(8, 2)], yt.at[:, pl.ds(0, 2)], right),
-        remote(yt.at[:, pl.ds(2, 2)], yt.at[:, pl.ds(10, 2)], left),
-    ]
     lat_pass(yr, 2, acc)
 
     landed(zp.at[pl.ds(0, 15)], n_zp)
@@ -574,13 +574,14 @@
         compiler_params=pltpu.CompilerParams(
             collective_id=0, has_side_effects=True, vmem_limit_bytes=40 << 20
         ),
-    )(state, footpoints, conductance, inverse_blocks)
+    )(*(pltpu.with_memory_space_constraint(a, pltpu.HBM) for a in (state, footpoints, conductance, inverse_blocks)))
     return pl.pallas_call(
         finish,
         out_shape=whole + (jax.ShapeDtypeStruct((R, LON, LAT), F32),),
         in_specs=[vmem] * 4,
         out_specs=(hbm, hbm, hbm),
         scratch_shapes=[pltpu.VMEM((R, LON, LAT), F32), pltpu.SemaphoreType.DMA((3,))],
+        compiler_params=pltpu.CompilerParams(vmem_limit_bytes=8 << 20),
     )(cells, potential, table, footpoints)
 
 

time: 49 us -> 41.3 us (0.84)
  local copies, waits for them, and re-layouts: 4.74 us -> 0.01 us
  Pallas kernels: 43.3 us -> 40.6 us
    unnamed x14 -> x2, local copies, waits for them, and re-layouts: 4.74 us -> 0.01 us
    pallas_call x1, Pallas kernels: 41.4 us -> 39.7 us  [body(): pl.pallas_call(kernel, out_shape=whole + (jax.ShapeDtypeStruct((2, LAT),...]
    pallas_call x1, Pallas kernels: 1.88 us -> 0.84 us  [body(): pl.pallas_call(finish, out_shape=whole + (jax.ShapeDtypeStruct((R, LON, L...]
where the time goes in v3:
time: 41.3 us; the launch traced here: 41.2 us
  Pallas kernels  40.6 us (98%)
  between operations  0.65 us (2%)
    pallas_call x1, Pallas kernels, body(): pl.pallas_call(kernel, out_shape=whole + (jax.ShapeDtypeStruct((2, LAT),...  39.7 us
    pallas_call x1, Pallas kernels, body(): pl.pallas_call(finish, out_shape=whole + (jax.ShapeDtypeStruct((R, LON, L...  0.84 us

profile of v3, /device:TPU:1, one launch (start us, length us, event | category | flops | bytes accessed | tf_op | source)
XLA Modules:
  0.0 41.2 jit_solution(6508825691360952646)
XLA Ops:
  0.6 0.0 copy-start
  0.6 39.7 %shard_map.67 = (f32[8,16,8,128]{3,2,1,0:T(8,128)S(1)}, f32[1,128]{1,0:T(1,128)S(1)}, f32[2,128]{1,0:T(2,128)S(1)}) custom-call(f32[8,16,8,128]{3,2,1,0:T(8,128)} %state.1, s32[16,8,128]{2,1,0:T(8,128)} %foot.1, f32[4,1,128]{2,1,0:T(1,128)} %cond.1, f32[1,1,128,128]{3,2,1,0:T(8,128)} %inv.1), custom_call_target="tpu_custom_call" | custom-call | tf_op jit(solution)/shard_map/pallas_call | solution.py:541
  40.4 0.0 copy-done
  40.4 0.8 %shard_map.68 = (f32[8,16,8,128]{3,2,1,0:T(8,128)}, f32[1,128]{1,0:T(1,128)}, f32[16,8,128]{2,1,0:T(8,128)}) custom-call(f32[8,16,8,128]{3,2,1,0:T(8,128)S(1)} %get-tuple-element.6.state, f32[1,128]{1,0:T(1,128)S(1)} %get-tuple-element.7.pot, f32[2,128]{1,0:T(2,128)S(1)} %get-tuple-element.8.table, s32[16,8,128]{2,1,0:T(8,128)S(1)} %copy-done), custom_call_target="tpu_custom_call" | custom-call | tf_op jit(solution)/shard_map/pallas_call | solution.py:578
Async XLA Ops:
  0.6 39.7 %copy-start = (s32[16,8,128]{2,1,0:T(8,128)S(1)}, s32[16,8,128]{2,1,0:T(8,128)}, u32[]{:S(2)}) copy-start(s32[16,8,128]{2,1,0:T(8,128)} %foot.1) | copy-start | bytes 196612

commit v4 on v2

--- a/solution.py
+++ b/solution.py
@@ -73,14 +73,14 @@
 
 
 def lat_pass(src, base, acc):
-    lane = lax.broadcasted_iota(jnp.int32, (2, LON, LAT), 2)
+    lane = lax.broadcasted_iota(jnp.int32, (4, LON, LAT), 2)
     last, first = lane == LAT - 1, lane == 0
 
     def step(i, carry):
-        l = i * 2
+        l = i * 4
         left, right = [], []
         for v in range(8):
-            u = src[v, pl.ds(base + l, 2)]
+            u = src[v, pl.ds(base + l, 4)]
             d = jnp.where(last, 0.0, pltpu.roll(u, LAT - 1, 2) - u)
             h = 0.5 * minmod(d, pltpu.roll(d, 1, 2))
             left.append(u + h)
@@ -93,13 +93,13 @@
             jump = top * (right[v] - left[v])
             if fl[v] is None:
                 f = -jump
-                acc[v, pl.ds(l, 2)] = f - jnp.where(first, 0.0, pltpu.roll(f, 1, 2))
+                acc[v, pl.ds(l, 4)] = f - jnp.where(first, 0.0, pltpu.roll(f, 1, 2))
             else:
                 f = (fl[v] + fr[v]) - jump
-                acc[v, pl.ds(l, 2)] = f - jnp.where(first, 2.0 * fl[v], pltpu.roll(f, 1, 2))
+                acc[v, pl.ds(l, 4)] = f - jnp.where(first, 2.0 * fl[v], pltpu.roll(f, 1, 2))
         return carry
 
-    lax.fori_loop(0, R // 2, step, 0)
+    lax.fori_loop(0, R // 4, step, 0)
 
 
 def radial_pass(ext, acc):
@@ -185,6 +185,8 @@
     right = ((s + 1) % ring, h)
     left = ((s + ring - 1) % ring, h)
     mate = (s, 1 - h)
+    right2 = ((s + 2) % ring, h)
+    left2 = ((s + ring - 2) % ring, h)
     line = [(base + (z + k) % NZ, c) for k in FAR_FIRST_Z for c in (0, 1)] + [mate]
     plane = [((xy + k) % NXY, ((xy + k) % NXY * NZ + z, h)) for k in FAR_FIRST_XY]
     slot = z * 2 + h
@@ -210,7 +212,7 @@
         pltpu.make_async_copy(ref, ref, send_sem.at[n]).wait()
 
     barrier = pltpu.get_barrier_semaphore()
-    partners = line + [p for _, p in plane] + [right, left]
+    partners = [p for _, p in plane[:5]] + line[:6] + [right2, left2, right, left] + [p for _, p in plane[5:]] + line[6:]
     for device in partners:
         pl.semaphore_signal(barrier, inc=1, device_id=device, device_id_type=MESH)
 
@@ -230,27 +232,32 @@
         for j in range(LON):
             dst[v, j + 2] = src[v, 2 : R + 2, j, :]
 
-    loads[0].wait()
-    for v in (4, 6):
-        turn(xt, xr, v)
     pl.semaphore_wait(barrier, len(partners))
 
     edge, low = 18 * h, 14 * (1 - h)
     copies, near = [], []
     for k, v in enumerate((6, 4)):
-        near.append(remote(xt.at[v, 9], edge_in.at[k, 0], right))
-        near.append(remote(xt.at[v, 2], edge_in.at[k, 1], left))
+        near.append(remote(state.at[v, :, LON - 1, :], edge_in.at[k, 0], right))
+        near.append(remote(state.at[v, :, 0, :], edge_in.at[k, 1], left))
     near.append(remote(state.at[pl.ds(4, 3), pl.ds(low, 2)], xr.at[pl.ds(4, 3), pl.ds(edge, 2)], mate))
 
     own_block, own_cond = inv.at[0, 0], cond
     go_right = [remote(own_cond, conds.at[2, 0], right), remote(own_block, blocks.at[2, 0], right)]
     go_left = [remote(own_cond, conds.at[4, 0], left), remote(own_block, blocks.at[4, 0], left)]
     go_mate = [remote(own_cond, conds.at[3, 1], mate), remote(own_block, blocks.at[3, 1], mate)]
+    for j in (0, 1):
+        copies.append(remote(state.at[:, :, 6 + j, :], xt.at[:, j], right))
+        copies.append(remote(state.at[:, :, j, :], xt.at[:, 10 + j], left))
+    hop_right = [remote(own_cond, conds.at[1, 0], right2), remote(own_block, blocks.at[1, 0], right2)]
+    hop_left = [remote(own_cond, conds.at[5, 0], left2), remote(own_block, blocks.at[5, 0], left2)]
     side = [
         remote(state.at[pl.ds(0, 4), pl.ds(low, 2)], xr.at[pl.ds(0, 4), pl.ds(edge, 2)], mate),
         remote(state.at[pl.ds(7, 1), pl.ds(low, 2)], xr.at[pl.ds(7, 1), pl.ds(edge, 2)], mate),
     ]
 
+    loads[0].wait()
+    for v in (4, 6):
+        turn(xt, xr, v)
     loads[1].wait()
     loads[2].wait()
     for v in (5, 0, 1, 2, 3, 7):
@@ -322,14 +329,8 @@
     for device in line:
         remote(part, zb.at[slot], device, n_zb)
 
-    copies += [
-        remote(xt.at[:, pl.ds(8, 2)], xt.at[:, pl.ds(0, 2)], right),
-        remote(xt.at[:, pl.ds(2, 2)], xt.at[:, pl.ds(10, 2)], left),
-    ]
     for c in go_right + go_left + go_mate + side:
         c.wait_recv()
-    hop_right = [remote(conds.at[2, 0], conds.at[1, 0], right), remote(blocks.at[2, 0], blocks.at[1, 0], right)]
-    hop_left = [remote(conds.at[4, 0], conds.at[5, 0], left), remote(blocks.at[4, 0], blocks.at[5, 0], left)]
     hop_mate = [
         remote(conds.at[2, 0], conds.at[2, 1], mate), remote(blocks.at[2, 0], blocks.at[2, 1], mate),
         remote(conds.at[4, 0], conds.at[4, 1], mate), remote(blocks.at[4, 0], blocks.at[4, 1], mate),
@@ -386,27 +387,28 @@
     green[3, 0] = blocks[3, 0]
     widen(lambda d, c: blocks.at[d + 3, c], qb, 0)
     radial_pass(xr, acc)
-
+    for c in hop_right + hop_left:
+        c.wait_recv()
+    end_right = [remote(blocks.at[1, 0], blocks.at[0, 0], right)]
+    end_left = [remote(blocks.at[5, 0], blocks.at[6, 0], left)]
+    end_mate = [remote(blocks.at[1, 0], blocks.at[1, 1], mate), remote(blocks.at[5, 0], blocks.at[5, 1], mate)]
+    row128 = lax.broadcasted_iota(jnp.int32, (LAT, LAT), 0)
+    lane128 = lax.broadcasted_iota(jnp.int32, (LAT, LAT), 1)
+    pick = jnp.where(lane128 == row128 + (z - REACH), 1.0, 0.0).astype(BF16)
     landed(zb.at[pl.ds(0, 15)], n_zb)
     columns = jnp.concatenate([zb[2 * k] + zb[2 * k + 1] for k in range(NZ)], axis=0)
-    row128 = lax.broadcasted_iota(jnp.int32, (LAT, LAT), 0)
-    lane128 = lax.broadcasted_iota(jnp.int32, (LAT, LAT), 1)
-    placed = jnp.where(
-        jnp.right_shift(row128, 4) == xy % 8, jnp.concatenate([columns] * 8, axis=0), 0.0
-    )
-    pick = jnp.where(lane128 == row128 + (z - REACH), 1.0, 0.0).astype(BF16)
-    p_hi, p_lo = split2(placed)
-    a1s[...] = (nt(pick, p_hi) + nt(pick, p_lo)).reshape(NXY, 8, LAT)
+    p_hi, p_lo = split2(columns)
+    seven = nt(pick, p_hi) + nt(pick, p_lo)
+    seven = jnp.concatenate([seven, jnp.zeros((LAT, LAT - 16), F32)], axis=1)
+    a1s[...] = pltpu.roll(seven, (xy % 8) * 16, 1).reshape(NXY, 8, LAT)
     n_a1 = fresh()
     for to, device in plane:
         remote(a1s.at[to], a1.at[xy], device, n_a1)
     a1[xy] = a1s[xy]
 
-    for c in hop_right + hop_left + hop_mate:
+
+    for c in hop_mate:
         c.wait_recv()
-    end_right = [remote(blocks.at[1, 0], blocks.at[0, 0], right)]
-    end_left = [remote(blocks.at[5, 0], blocks.at[6, 0], left)]
-    end_mate = [remote(blocks.at[1, 0], blocks.at[1, 1], mate), remote(blocks.at[5, 0], blocks.at[5, 1], mate)]
     widen(lambda d, c: qb.at[d + 3, c], qa, 1)
     for c in copies:
         c.wait_recv()
@@ -423,6 +425,11 @@
         e = yr[v, 2 + 15 * h]
         yr[v, edge] = e
         yr[v, edge + 1] = e
+    again = [
+        remote(yr.at[:, pl.ds(2 + low, 2)], yr.at[:, pl.ds(edge, 2)], mate),
+        remote(yt.at[:, pl.ds(8, 2)], yt.at[:, pl.ds(0, 2)], right),
+        remote(yt.at[:, pl.ds(2, 2)], yt.at[:, pl.ds(10, 2)], left),
+    ]
     for c in end_right + end_left + end_mate:
         c.wait_recv()
     widen(lambda d, c: qa.at[d + 3, c], None, 2)
@@ -446,26 +453,21 @@
     for device in line:
         remote(prow, zp.at[slot], device, n_zp)
 
-    again = [
-        remote(yr.at[:, pl.ds(2 + low, 2)], yr.at[:, pl.ds(edge, 2)], mate),
-        remote(yt.at[:, pl.ds(8, 2)], yt.at[:, pl.ds(0, 2)], right),
-        remote(yt.at[:, pl.ds(2, 2)], yt.at[:, pl.ds(10, 2)], left),
-    ]
     lat_pass(yr, 2, acc)
 
-    landed(zp.at[pl.ds(0, 15)], n_zp)
-    lines = jnp.concatenate(
-        [jnp.concatenate([zp[2 * k], zp[2 * k + 1]], axis=1) for k in range(NZ)], axis=0
-    )
-    row256 = lax.broadcasted_iota(jnp.int32, (LAT, 2 * LAT), 0)
-    placed = jnp.where(jnp.right_shift(row256, 3) == xy, jnp.concatenate([lines] * NXY, axis=0), 0.0)
     m = lax.broadcasted_iota(jnp.int32, (2 * NXY, 2 * LAT), 0)
     n = lax.broadcasted_iota(jnp.int32, (2 * NXY, 2 * LAT), 1)
     pick2 = jnp.where(
         n == 2 * (jnp.right_shift(m, 1) * NZ + z) + jnp.bitwise_and(m, 1), 1.0, 0.0
     ).astype(BF16)
-    l_hi, l_lo = split2(placed)
+    landed(zp.at[pl.ds(0, 15)], n_zp)
+    lines = jnp.concatenate(
+        [jnp.concatenate([zp[2 * k], zp[2 * k + 1]], axis=1) for k in range(NZ)], axis=0
+    )
+    l_hi, l_lo = split2(lines)
     picked = nt(pick2, l_hi) + nt(pick2, l_lo)
+    picked = jnp.concatenate([picked, jnp.zeros((2 * NXY, LAT - NZ), F32)], axis=1)
+    picked = pltpu.roll(picked, xy * NZ, 1)
     for k in range(NXY):
         a2s[k] = picked[2 * k : 2 * k + 2]
     n_a2 = fresh()
@@ -528,7 +530,7 @@
         c.wait()
 
 
-N_SEMS = 48
+N_SEMS = 52
 
 
 def body(state, footpoints, conductance, inverse_blocks):
@@ -574,13 +576,14 @@
         compiler_params=pltpu.CompilerParams(
             collective_id=0, has_side_effects=True, vmem_limit_bytes=40 << 20
         ),
-    )(state, footpoints, conductance, inverse_blocks)
+    )(*(pltpu.with_memory_space_constraint(a, pltpu.HBM) for a in (state, footpoints, conductance, inverse_blocks)))
     return pl.pallas_call(
         finish,
         out_shape=whole + (jax.ShapeDtypeStruct((R, LON, LAT), F32),),
         in_specs=[vmem] * 4,
         out_specs=(hbm, hbm, hbm),
         scratch_shapes=[pltpu.VMEM((R, LON, LAT), F32), pltpu.SemaphoreType.DMA((3,))],
+        compiler_params=pltpu.CompilerParams(vmem_limit_bytes=8 << 20),
     )(cells, potential, table, footpoints)
 
 

time: 49 us -> 39.4 us (0.80)
  local copies, waits for them, and re-layouts: 4.74 us -> 0.01 us
  Pallas kernels: 43.3 us -> 38.7 us
    unnamed x14 -> x2, local copies, waits for them, and re-layouts: 4.74 us -> 0.01 us
    pallas_call x1, Pallas kernels: 41.4 us -> 37.8 us  [body(): pl.pallas_call(kernel, out_shape=whole + (jax.ShapeDtypeStruct((2, LAT),...]
    pallas_call x1, Pallas kernels: 1.88 us -> 0.84 us  [body(): pl.pallas_call(finish, out_shape=whole + (jax.ShapeDtypeStruct((R, LON, L...]
where the time goes in v4:
time: 39.4 us; the launch traced here: 39.3 us
  Pallas kernels  38.7 us (98%)
  between operations  0.65 us (2%)
    pallas_call x1, Pallas kernels, body(): pl.pallas_call(kernel, out_shape=whole + (jax.ShapeDtypeStruct((2, LAT),...  37.8 us
    pallas_call x1, Pallas kernels, body(): pl.pallas_call(finish, out_shape=whole + (jax.ShapeDtypeStruct((R, LON, L...  0.84 us

profile of v4, /device:TPU:1, one launch (start us, length us, event | category | flops | bytes accessed | tf_op | source)
XLA Modules:
  0.0 39.3 jit_solution(10065084785471090059)
XLA Ops:
  0.6 0.0 copy-start
  0.6 37.8 %shard_map.67 = (f32[8,16,8,128]{3,2,1,0:T(8,128)S(1)}, f32[1,128]{1,0:T(1,128)S(1)}, f32[2,128]{1,0:T(2,128)S(1)}) custom-call(f32[8,16,8,128]{3,2,1,0:T(8,128)} %state.1, s32[16,8,128]{2,1,0:T(8,128)} %foot.1, f32[4,1,128]{2,1,0:T(1,128)} %cond.1, f32[1,1,128,128]{3,2,1,0:T(8,128)} %inv.1), custom_call_target="tpu_custom_call" | custom-call | tf_op jit(solution)/shard_map/pallas_call | solution.py:543
  38.5 0.0 copy-done
  38.5 0.8 %shard_map.68 = (f32[8,16,8,128]{3,2,1,0:T(8,128)}, f32[1,128]{1,0:T(1,128)}, f32[16,8,128]{2,1,0:T(8,128)}) custom-call(f32[8,16,8,128]{3,2,1,0:T(8,128)S(1)} %get-tuple-element.6.state, f32[1,128]{1,0:T(1,128)S(1)} %get-tuple-element.7.pot, f32[2,128]{1,0:T(2,128)S(1)} %get-tuple-element.8.table, s32[16,8,128]{2,1,0:T(8,128)S(1)} %copy-done), custom_call_target="tpu_custom_call" | custom-call | tf_op jit(solution)/shard_map/pallas_call | solution.py:580
Async XLA Ops:
  0.6 37.8 %copy-start = (s32[16,8,128]{2,1,0:T(8,128)S(1)}, s32[16,8,128]{2,1,0:T(8,128)}, u32[]{:S(2)}) copy-start(s32[16,8,128]{2,1,0:T(8,128)} %foot.1) | copy-start | bytes 196612

commit v5 on v4

--- a/solution.py
+++ b/solution.py
@@ -386,7 +386,6 @@
 
     green[3, 0] = blocks[3, 0]
     widen(lambda d, c: blocks.at[d + 3, c], qb, 0)
-    radial_pass(xr, acc)
     for c in hop_right + hop_left:
         c.wait_recv()
     end_right = [remote(blocks.at[1, 0], blocks.at[0, 0], right)]
@@ -410,6 +409,7 @@
     for c in hop_mate:
         c.wait_recv()
     widen(lambda d, c: qb.at[d + 3, c], qa, 1)
+    radial_pass(xr, acc)
     for c in copies:
         c.wait_recv()
     lon_pass(xt, acct)

time: 39.4 us -> 39.4 us (level)
  no operation moved by 1% of the time
where the time goes in v5:
time: 39.4 us; the launch traced here: 39.3 us
  Pallas kernels  38.7 us (98%)
  between operations  0.65 us (2%)
    pallas_call x1, Pallas kernels, body(): pl.pallas_call(kernel, out_shape=whole + (jax.ShapeDtypeStruct((2, LAT),...  37.8 us
    pallas_call x1, Pallas kernels, body(): pl.pallas_call(finish, out_shape=whole + (jax.ShapeDtypeStruct((R, LON, L...  0.84 us

profile of v5, /device:TPU:1, one launch (start us, length us, event | category | flops | bytes accessed | tf_op | source)
XLA Modules:
  0.0 39.3 jit_solution(9434909434810301616)
XLA Ops:
  0.6 0.0 copy-start
  0.6 37.8 %shard_map.67 = (f32[8,16,8,128]{3,2,1,0:T(8,128)S(1)}, f32[1,128]{1,0:T(1,128)S(1)}, f32[2,128]{1,0:T(2,128)S(1)}) custom-call(f32[8,16,8,128]{3,2,1,0:T(8,128)} %state.1, s32[16,8,128]{2,1,0:T(8,128)} %foot.1, f32[4,1,128]{2,1,0:T(1,128)} %cond.1, f32[1,1,128,128]{3,2,1,0:T(8,128)} %inv.1), custom_call_target="tpu_custom_call" | custom-call | tf_op jit(solution)/shard_map/pallas_call | solution.py:543
  38.5 0.0 copy-done
  38.5 0.8 %shard_map.68 = (f32[8,16,8,128]{3,2,1,0:T(8,128)}, f32[1,128]{1,0:T(1,128)}, f32[16,8,128]{2,1,0:T(8,128)}) custom-call(f32[8,16,8,128]{3,2,1,0:T(8,128)S(1)} %get-tuple-element.6.state, f32[1,128]{1,0:T(1,128)S(1)} %get-tuple-element.7.pot, f32[2,128]{1,0:T(2,128)S(1)} %get-tuple-element.8.table, s32[16,8,128]{2,1,0:T(8,128)S(1)} %copy-done), custom_call_target="tpu_custom_call" | custom-call | tf_op jit(solution)/shard_map/pallas_call | solution.py:580
Async XLA Ops:
  0.6 37.8 %copy-start = (s32[16,8,128]{2,1,0:T(8,128)S(1)}, s32[16,8,128]{2,1,0:T(8,128)}, u32[]{:S(2)}) copy-start(s32[16,8,128]{2,1,0:T(8,128)} %foot.1) | copy-start | bytes 196612
